TPU v7x, 256 devices: a whole 4x4x8 slice. The times are simulated.
256 devices in a mesh: row: 32 (over x_lo, z, core), col: 8 (over y, x_hi).
Axes of the slice: x: 4 (x_hi: 2, x_lo: 2; x = x_hi * 2 + x_lo), y: 4, z: 8, core: 2. Of those that a mesh axis runs over, the one named last changes fastest.
Arguments:
- maps: bfloat16 [48, 1024, 1024], P(None, 'row', 'col'), may hold values from -6 to 6
- kernel: bfloat16 [3, 3, 48, 48], replicated, may hold values from -0.3125 to 0.3125
- mixing: bfloat16 [48, 48], replicated, may hold values from -0.875 to 0.875
- cotangent: bfloat16 [48, 1024, 1024], P(None, 'row', 'col'), may hold values from -6 to 6
Outputs:
- output: bfloat16 [48, 1024, 1024], P(None, 'row', 'col')
- grad_maps: bfloat16 [48, 1024, 1024], P(None, 'row', 'col')
- grad_kernel: float32 [3, 3, 48, 48], replicated
- grad_mixing: float32 [48, 48], replicated
All inputs are finite; a program needn't handle non-finite values.
Results may differ from a plain program's by a relative error of at most 0.0056.
Values may be sent and summed in bfloat16 or wider, within the bound.
A program may use at most 128 MiB of HBM per device.

v0:
```python
import jax
import jax.numpy as jnp
from jax import lax
from jax.sharding import PartitionSpec as P

DILATION = 8


def with_halo(array, sides, width):
    for axis, dim in sides:
        peers, length = (lax.axis_size(axis), array.shape[dim])
        up = [(i, (i + 1) % peers) for i in range(peers - 1)]
        down = [(j, i) for i, j in up]
        last = lax.slice_in_dim(array, length - width, length, axis=dim)
        initial = lax.slice_in_dim(array, 0, width, axis=dim)
        before = lax.ppermute(last, axis, up)
        after = lax.ppermute(initial, axis, down)
        array = jnp.concatenate([before, array, after], axis=dim)
    return array


def mirror_tile(tile):
    row_count = lax.axis_size("row")
    col_count = lax.axis_size("col")
    chans, rows, cols = tile.shape
    width = rows // col_count
    strip = lax.all_to_all(tile, "col", split_axis=1, concat_axis=2, tiled=True)
    blocks = lax.all_to_all(strip, "row", split_axis=2, concat_axis=1, tiled=True)
    turned = jnp.transpose(blocks.reshape(chans, row_count, width, rows), (0, 3, 1, 2))
    landed = lax.all_to_all(turned, "col", split_axis=2, concat_axis=3, tiled=True)
    return landed.reshape(chans, rows, cols)


def window(padded, top, left, rows, cols):
    return padded[:, top : top + rows, left : left + cols]


def shards(maps, kernel, mixing, cotangent):
    chans, rows, cols = maps.shape
    map_bins = rows * lax.axis_size("row")
    active = jnp.maximum(maps, 0)
    padded = with_halo(active, (("row", 1), ("col", 2)), DILATION)
    before = jnp.zeros((chans, rows, cols), jnp.float32)
    for row_tap in range(3):
        for col_tap in range(3):
            piece = window(padded, DILATION * row_tap, DILATION * col_tap, rows, cols)
            before = before + jnp.einsum(
                "io,ihw->ohw", kernel[row_tap, col_tap], piece, preferred_element_type=jnp.float32
            )
    hidden = jnp.maximum(before, 0.0).astype(jnp.bfloat16)
    mixed = jnp.einsum("io,ihw->ohw", mixing, hidden, preferred_element_type=jnp.float32).astype(
        jnp.bfloat16
    )
    mixed_turned = mirror_tile(mixed)
    grad_turned = mirror_tile(cotangent)
    output = (
        maps.astype(jnp.float32)
        + 0.5 * (mixed.astype(jnp.float32) + mixed_turned.astype(jnp.float32))
    ).astype(jnp.bfloat16)
    grad_wide = cotangent.astype(jnp.float32)
    grad_mixed = (0.5 * (grad_wide + grad_turned.astype(jnp.float32))).astype(jnp.bfloat16)
    local_mixing = jnp.einsum("ihw,ohw->io", hidden, grad_mixed, preferred_element_type=jnp.float32)
    grad_hidden = jnp.einsum("io,ohw->ihw", mixing, grad_mixed, preferred_element_type=jnp.float32)
    grad_before = jnp.where(hidden > 0, grad_hidden, 0.0).astype(jnp.bfloat16)
    tap_grads = []
    for row_tap in range(3):
        for col_tap in range(3):
            piece = window(padded, DILATION * row_tap, DILATION * col_tap, rows, cols)
            tap_grads.append(
                jnp.einsum("ihw,ohw->io", piece, grad_before, preferred_element_type=jnp.float32)
            )
    local_kernel = jnp.stack(tap_grads).reshape(3, 3, chans, chans)
    grad_kernel, grad_mixing = lax.psum((local_kernel, local_mixing), ("row", "col"))
    grad_padded = with_halo(grad_before, (("row", 1), ("col", 2)), DILATION)
    grad_active = jnp.zeros((chans, rows, cols), jnp.float32)
    for row_tap in range(3):
        for col_tap in range(3):
            piece = window(
                grad_padded,
                2 * DILATION - DILATION * row_tap,
                2 * DILATION - DILATION * col_tap,
                rows,
                cols,
            )
            grad_active = grad_active + jnp.einsum(
                "io,ohw->ihw", kernel[row_tap, col_tap], piece, preferred_element_type=jnp.float32
            )
    grad_maps = (grad_wide + jnp.where(maps > 0, grad_active, 0.0)).astype(jnp.bfloat16)
    return (output, grad_maps, grad_kernel / map_bins, grad_mixing / map_bins)


def solution(mesh):
    placed = (P(None, "row", "col"), P(), P(), P(None, "row", "col"))
    return jax.shard_map(
        shards,
        mesh=mesh,
        in_specs=placed,
        out_specs=(P(None, "row", "col"), P(None, "row", "col"), P(), P()),
        check_vma=False,
    )
```

profile of v0, /device:TPU:6, one launch (start us, length us, event | category | flops | bytes accessed | tf_op | source)
XLA Modules:
  0.0 491.1 jit_solution(16474281042866536680)
XLA Ops:
  7.2 1.2 copy_maximum_fusion
  8.4 1.9 collective-permute-start
  10.3 7.5 %collective-permute-start.1 = (bf16[48,8,128]{2,0,1:T(8,128)(2,1)S(1)}, bf16[48,8,128]{2,0,1:T(8,128)(2,1)S(1)}, u32[]{:S(2)}, u32[]{:S(2)}) collective-permute-start(bf16[48,8,128]{2,0,1:T(8,128)(2,1)S(1)} %get-tuple-element.27), channel_id=1, source_target_pairs={{8,0},{16,8},{24,16},{32,24},{40,32},{48,40},{56,48},{64,56},{72,6... | collective-permute-start | bytes 294920 | tf_op jit(solution)/shard_map/ppermute | solution.py:17
  17.8 0.9 copy.88
  18.7 7.4 %all-to-all-start.3 = ((bf16[48,32,128]{2,0,1:T(8,128)(2,1)}), bf16[48,32,128]{2,0,1:T(8,128)(2,1)S(1)}, u32[]{:S(2)}, u32[]{:S(2)}) async-start(bf16[48,32,128]{2,0,1:T(8,128)(2,1)} %copy.88), calls=%async_computation.3 | async-start | bytes 786432 | tf_op jit(solution)/shard_map/all_to_all | solution.py:27
  26.5 0.5 copy.68
  27.0 0.5 copy.72
  27.5 1.9 collective-permute-start.3
  29.4 6.3 %collective-permute-start.2 = (bf16[48,48,8]{1,2,0:T(8,128)(2,1)S(1)}, bf16[48,48,8]{1,2,0:T(8,128)(2,1)S(1)}, u32[]{:S(2)}, u32[]{:S(2)}) collective-permute-start(bf16[48,48,8]{1,2,0:T(8,128)(2,1)S(1)} %copy.68), channel_id=1, source_target_pairs={{0,1},{1,2},{2,3},{3,4},{4,5},{5,6},{6,7},{8,9},{9,10},{10,11},{11... | collective-permute-start | bytes 110600 | tf_op jit(solution)/shard_map/ppermute | solution.py:16
  36.1 1.9 collective-permute-done.2
  38.0 0.5 copy.69
  38.5 0.5 copy.73
  39.0 0.8 maximum_maximum_fusion
  39.8 0.3 fusion.53
  40.4 0.3 convolution_add_fusion.11
  41.1 0.7 copy-done.3
  42.1 0.3 convolution_add_fusion.8
  43.1 0.8 copy-done.5
  43.8 1.1 fusion.12
  44.9 8.2 %all-to-all-start = ((bf16[48,32,128]{2,0,1:T(8,128)(2,1)}), bf16[48,32,128]{2,0,1:T(8,128)(2,1)S(1)}, u32[]{:S(2)}, u32[]{:S(2)}) async-start(bf16[48,32,128]{2,0,1:T(8,128)(2,1)} %fusion.12), calls=%async_computation | async-start | bytes 786432 | tf_op jit(solution)/shard_map/all_to_all | solution.py:27
  53.0 0.7 copy.91
  53.7 2.5 reshape.66
  56.2 3.7 all-to-all-done
  59.8 7.5 %all-to-all-start.4 = ((bf16[32,2,3072]{2,1,0:T(2,128)(2,1)}), bf16[32,2,3072]{2,1,0:T(2,128)(2,1)S(1)}, u32[]{:S(2)}, u32[]{:S(2)}) async-start(bf16[32,2,3072]{2,1,0:T(2,128)(2,1)} %reshape.66), calls=%async_computation.4 | async-start | bytes 786432 | tf_op jit(solution)/shard_map/all_to_all | solution.py:28
  67.3 0.7 copy.122
  68.0 2.5 reshape.62
  70.5 11.4 %all-to-all-done.4 = bf16[32,2,3072]{2,1,0:T(2,128)(2,1)S(1)} async-done(((bf16[32,2,3072]{2,1,0:T(2,128)(2,1)}), bf16[32,2,3072]{2,1,0:T(2,128)(2,1)S(1)}, u32[]{:S(2)}, u32[]{:S(2)}) %all-to-all-start.4) | async-done | bytes 393248 | tf_op jit(solution)/shard_map/all_to_all | solution.py:28
  81.9 5.2 %all-to-all-start.1 = ((bf16[32,2,3072]{2,1,0:T(2,128)(2,1)}), bf16[32,2,3072]{2,1,0:T(2,128)(2,1)S(1)}, u32[]{:S(2)}, u32[]{:S(2)}) async-start(bf16[32,2,3072]{2,1,0:T(2,128)(2,1)} %reshape.62), calls=%async_computation.1 | async-start | bytes 786432 | tf_op jit(solution)/shard_map/all_to_all | solution.py:28
  87.1 1.1 reshape.67
  88.3 2.3 reshape.68
  90.6 10.8 %all-to-all-done.1 = bf16[32,2,3072]{2,1,0:T(2,128)(2,1)S(1)} async-done(((bf16[32,2,3072]{2,1,0:T(2,128)(2,1)}), bf16[32,2,3072]{2,1,0:T(2,128)(2,1)S(1)}, u32[]{:S(2)}, u32[]{:S(2)}) %all-to-all-start.1) | async-done | bytes 393248 | tf_op jit(solution)/shard_map/all_to_all | solution.py:28
  101.5 6.0 %all-to-all-start.5 = ((bf16[8,2,12288]{2,1,0:T(2,128)(2,1)}), bf16[8,2,12288]{2,1,0:T(2,128)(2,1)S(1)}, u32[]{:S(2)}, u32[]{:S(2)}) async-start(bf16[8,2,12288]{2,1,0:T(2,128)(2,1)} %reshape.68), calls=%async_computation.5 | async-start | bytes 786432 | tf_op jit(solution)/shard_map/all_to_all | solution.py:30
  107.5 1.1 reshape.63
  108.8 2.3 reshape.64
  111.1 3.2 all-to-all-done.5
  114.3 6.7 %all-to-all-start.2 = ((bf16[8,2,12288]{2,1,0:T(2,128)(2,1)}), bf16[8,2,12288]{2,1,0:T(2,128)(2,1)}, u32[]{:S(2)}, u32[]{:S(2)}) async-start(bf16[8,2,12288]{2,1,0:T(2,128)(2,1)} %reshape.64), calls=%async_computation.2 | async-start | bytes 786432 | tf_op jit(solution)/shard_map/all_to_all | solution.py:30
  121.0 1.1 reshape.69
  122.6 1.3 copy.95
  123.9 1.6 convolution_bitcast_fusion.3
  125.9 1.3 fusion.21
  127.2 73.6 %psum.15 = f32[48,48]{1,0:T(8,128)S(1)} all-reduce(f32[48,48]{1,0:T(8,128)S(1)} %convolution_bitcast_fusion.3), channel_id=1, replica_groups=mesh['row'=32,'col'=8] {'row','col'}, use_global_device_ids=true, to_apply=%region_1.2 | all-reduce | flops 2304 | bytes 18432 | tf_op jit(solution)/shard_map/psum | solution.py:73
  201.4 0.7 copy-done.10
  203.8 0.7 copy-done.13
  204.5 0.6 broadcast_multiply_fusion.1
  205.1 1.9 collective-permute-start.4
  207.0 6.0 %collective-permute-start.5 = (bf16[48,8,128]{2,0,1:T(8,128)(2,1)S(1)}, bf16[48,8,128]{2,0,1:T(8,128)(2,1)S(1)}, u32[]{:S(2)}, u32[]{:S(2)}) collective-permute-start(bf16[48,8,128]{2,0,1:T(8,128)(2,1)S(1)} %get-tuple-element.25), channel_id=1, source_target_pairs={{8,0},{16,8},{24,16},{32,24},{40,32},{48,40},{56,48},{64,56},{72,6... | collective-permute-start | bytes 294920 | tf_op jit(solution)/shard_map/ppermute | solution.py:17
  213.0 240.1 %all-reduce.2.cloned.1.call-done = f32[3,3,48,48]{3,2,1,0:T(8,128)} async-done(((f32[3,3,48,48]{3,2,1,0:T(8,128)}), f32[3,3,48,48]{3,2,1,0:T(8,128)}) %all-reduce.2.cloned.1.call-update) | async-done | bytes 82960 | tf_op jit(solution)/shard_map/psum | solution.py:73
  453.1 1.6 broadcast_multiply_fusion
  455.1 0.5 copy.96
  455.6 0.5 copy.100
  456.1 4.3 collective-permute-start.7
  460.4 3.1 collective-permute-start.6
  463.9 5.3 %collective-permute-done.6 = bf16[48,48,8]{1,2,0:T(8,128)(2,1)S(1)} collective-permute-done((bf16[48,48,8]{1,2,0:T(8,128)(2,1)S(1)}, bf16[48,48,8]{1,2,0:T(8,128)(2,1)S(1)}, u32[]{:S(2)}, u32[]{:S(2)}) %collective-permute-start.6) | collective-permute-done | bytes 36896 | tf_op jit(solution)/shard_map/ppermute | solution.py:17
  469.3 1.3 copy.97
  470.6 1.3 copy.101
  471.9 2.0 pad_maximum_fusion.1
  473.9 0.3 convolution_add_fusion.5
  474.4 0.3 convolution_add_fusion.3
  475.5 0.6 fusion.9
  476.1 0.8 copy.110
  476.9 2.3 reshape.65
  479.7 2.2 copy.87
  481.9 1.5 add_convert_fusion
  483.4 0.8 copy.109
  (67 shorter events, 7.9 us)
Async XLA Ops:
  7.2 36.7 %copy-start = (bf16[48,48]{1,0:T(8,128)(2,1)S(1)}, bf16[48,48]{1,0:T(8,128)(2,1)}, u32[]{:S(2)}) copy-start(bf16[48,48]{1,0:T(8,128)(2,1)} %param.6) | copy-start | bytes 13828
  7.2 10.6 %copy-start.1 = (bf16[48,32,128]{2,1,0:T(8,128)(2,1)S(1)}, bf16[48,32,128]{2,1,0:T(8,128)(2,1)}, u32[]{:S(2)}) copy-start(bf16[48,32,128]{2,1,0:T(8,128)(2,1)} %param.7) | copy-start | bytes 1179652
  8.4 17.8 %collective-permute-start = (bf16[48,8,128]{2,0,1:T(8,128)(2,1)S(1)}, bf16[48,8,128]{2,0,1:T(8,128)(2,1)S(1)}, u32[]{:S(2)}, u32[]{:S(2)}) collective-permute-start(bf16[48,8,128]{2,0,1:T(8,128)(2,1)S(1)} %get-tuple-element.26), channel_id=1, source_target_pairs={{0,8},{8,16},{16,24},{24,32},{32,40},{40,48},{48,56},{56,64},{64,7... | collective-permute-start | bytes 294920 | tf_op jit(solution)/shard_map/ppermute | solution.py:16
  10.3 15.8 %collective-permute-start.1 = (bf16[48,8,128]{2,0,1:T(8,128)(2,1)S(1)}, bf16[48,8,128]{2,0,1:T(8,128)(2,1)S(1)}, u32[]{:S(2)}, u32[]{:S(2)}) collective-permute-start(bf16[48,8,128]{2,0,1:T(8,128)(2,1)S(1)} %get-tuple-element.27), channel_id=1, source_target_pairs={{8,0},{16,8},{24,16},{32,24},{40,32},{48,40},{56,48},{64,56},{72,6... | collective-permute-start | bytes 294920 | tf_op jit(solution)/shard_map/ppermute | solution.py:17
  18.7 26.2 %all-to-all-start.3 = ((bf16[48,32,128]{2,0,1:T(8,128)(2,1)}), bf16[48,32,128]{2,0,1:T(8,128)(2,1)S(1)}, u32[]{:S(2)}, u32[]{:S(2)}) async-start(bf16[48,32,128]{2,0,1:T(8,128)(2,1)} %copy.88), calls=%async_computation.3 | async-start | bytes 786432 | tf_op jit(solution)/shard_map/all_to_all | solution.py:27
  26.5 9.3 %copy-start.11 = (bf16[3,3,48,48]{3,2,1,0:T(8,128)(2,1)S(1)}, bf16[3,3,48,48]{3,2,1,0:T(8,128)(2,1)}, u32[]{:S(2)}) copy-start(bf16[3,3,48,48]{3,2,1,0:T(8,128)(2,1)} %param.5) | copy-start | bytes 124420
  27.5 10.9 %collective-permute-start.3 = (bf16[48,48,8]{1,2,0:T(8,128)(2,1)S(1)}, bf16[48,48,8]{1,2,0:T(8,128)(2,1)S(1)}, u32[]{:S(2)}, u32[]{:S(2)}) collective-permute-start(bf16[48,48,8]{1,2,0:T(8,128)(2,1)S(1)} %copy.72), channel_id=1, source_target_pairs={{1,0},{2,1},{3,2},{4,3},{5,4},{6,5},{7,6},{9,8},{10,9},{11,10},{12... | collective-permute-start | bytes 110600 | tf_op jit(solution)/shard_map/ppermute | solution.py:17
  29.4 8.5 %collective-permute-start.2 = (bf16[48,48,8]{1,2,0:T(8,128)(2,1)S(1)}, bf16[48,48,8]{1,2,0:T(8,128)(2,1)S(1)}, u32[]{:S(2)}, u32[]{:S(2)}) collective-permute-start(bf16[48,48,8]{1,2,0:T(8,128)(2,1)S(1)} %copy.68), channel_id=1, source_target_pairs={{0,1},{1,2},{2,3},{3,4},{4,5},{5,6},{6,7},{8,9},{9,10},{10,11},{11... | collective-permute-start | bytes 110600 | tf_op jit(solution)/shard_map/ppermute | solution.py:16
  39.8 2.3 copy-start.7
  39.8 2.6 copy-start.9
  40.8 1.0 copy-start.3
  43.0 0.8 copy-start.5
  44.9 15.0 %all-to-all-start = ((bf16[48,32,128]{2,0,1:T(8,128)(2,1)}), bf16[48,32,128]{2,0,1:T(8,128)(2,1)S(1)}, u32[]{:S(2)}, u32[]{:S(2)}) async-start(bf16[48,32,128]{2,0,1:T(8,128)(2,1)} %fusion.12), calls=%async_computation | async-start | bytes 786432 | tf_op jit(solution)/shard_map/all_to_all | solution.py:27
  59.8 22.0 %all-to-all-start.4 = ((bf16[32,2,3072]{2,1,0:T(2,128)(2,1)}), bf16[32,2,3072]{2,1,0:T(2,128)(2,1)S(1)}, u32[]{:S(2)}, u32[]{:S(2)}) async-start(bf16[32,2,3072]{2,1,0:T(2,128)(2,1)} %reshape.66), calls=%async_computation.4 | async-start | bytes 786432 | tf_op jit(solution)/shard_map/all_to_all | solution.py:28
  81.9 19.6 %all-to-all-start.1 = ((bf16[32,2,3072]{2,1,0:T(2,128)(2,1)}), bf16[32,2,3072]{2,1,0:T(2,128)(2,1)S(1)}, u32[]{:S(2)}, u32[]{:S(2)}) async-start(bf16[32,2,3072]{2,1,0:T(2,128)(2,1)} %reshape.62), calls=%async_computation.1 | async-start | bytes 786432 | tf_op jit(solution)/shard_map/all_to_all | solution.py:28
  101.5 12.9 %all-to-all-start.5 = ((bf16[8,2,12288]{2,1,0:T(2,128)(2,1)}), bf16[8,2,12288]{2,1,0:T(2,128)(2,1)S(1)}, u32[]{:S(2)}, u32[]{:S(2)}) async-start(bf16[8,2,12288]{2,1,0:T(2,128)(2,1)} %reshape.68), calls=%async_computation.5 | async-start | bytes 786432 | tf_op jit(solution)/shard_map/all_to_all | solution.py:30
  114.3 362.6 %all-to-all-start.2 = ((bf16[8,2,12288]{2,1,0:T(2,128)(2,1)}), bf16[8,2,12288]{2,1,0:T(2,128)(2,1)}, u32[]{:S(2)}, u32[]{:S(2)}) async-start(bf16[8,2,12288]{2,1,0:T(2,128)(2,1)} %reshape.64), calls=%async_computation.2 | async-start | bytes 786432 | tf_op jit(solution)/shard_map/all_to_all | solution.py:30
  121.0 332.1 %all-reduce.2.cloned.1.call-start = ((), (), s32[]{:S(2)}) async-start(), calls=%async_computation.6 | async-start | bytes 442368 | tf_op jit(solution)/shard_map/psum | solution.py:73
  123.9 1.6 copy-start.2
  123.9 1.6 copy-start.6
  125.8 75.2 %copy-start.8 = (bf16[48,48,136]{2,0,1:T(8,128)(2,1)S(1)}, bf16[48,48,136]{2,0,1:T(8,128)(2,1)}, u32[]{:S(2)}) copy-start(bf16[48,48,136]{2,0,1:T(8,128)(2,1)} %copy-done.7) | copy-start | bytes 1880068
  200.8 1.3 copy-start.10
  200.8 1.5 copy-start.4
  203.7 0.7 copy-start.13
  205.1 249.7 %collective-permute-start.4 = (bf16[48,8,128]{2,0,1:T(8,128)(2,1)S(1)}, bf16[48,8,128]{2,0,1:T(8,128)(2,1)S(1)}, u32[]{:S(2)}, u32[]{:S(2)}) collective-permute-start(bf16[48,8,128]{2,0,1:T(8,128)(2,1)S(1)} %get-tuple-element.24), channel_id=1, source_target_pairs={{0,8},{8,16},{16,24},{24,32},{32,40},{40,48},{48,56},{56,64},{64,7... | collective-permute-start | bytes 294920 | tf_op jit(solution)/shard_map/ppermute | solution.py:16
  207.0 247.7 %collective-permute-start.5 = (bf16[48,8,128]{2,0,1:T(8,128)(2,1)S(1)}, bf16[48,8,128]{2,0,1:T(8,128)(2,1)S(1)}, u32[]{:S(2)}, u32[]{:S(2)}) collective-permute-start(bf16[48,8,128]{2,0,1:T(8,128)(2,1)S(1)} %get-tuple-element.25), channel_id=1, source_target_pairs={{8,0},{16,8},{24,16},{32,24},{40,32},{48,40},{56,48},{64,56},{72,6... | collective-permute-start | bytes 294920 | tf_op jit(solution)/shard_map/ppermute | solution.py:17
  455.0 8.4 %copy-start.12 = (bf16[3,3,48,48]{3,2,1,0:T(8,128)(2,1)S(1)}, bf16[3,3,48,48]{3,2,1,0:T(8,128)(2,1)}, u32[]{:S(2)}) copy-start(bf16[3,3,48,48]{3,2,1,0:T(8,128)(2,1)} %param.5) | copy-start | bytes 124420
  456.1 14.5 %collective-permute-start.7 = (bf16[48,48,8]{1,2,0:T(8,128)(2,1)S(1)}, bf16[48,48,8]{1,2,0:T(8,128)(2,1)S(1)}, u32[]{:S(2)}, u32[]{:S(2)}) collective-permute-start(bf16[48,48,8]{1,2,0:T(8,128)(2,1)S(1)} %copy.100), channel_id=1, source_target_pairs={{0,1},{1,2},{2,3},{3,4},{4,5},{5,6},{6,7},{8,9},{9,10},{10,11},{11... | collective-permute-start | bytes 110600 | tf_op jit(solution)/shard_map/ppermute | solution.py:16
  460.4 8.9 %collective-permute-start.6 = (bf16[48,48,8]{1,2,0:T(8,128)(2,1)S(1)}, bf16[48,48,8]{1,2,0:T(8,128)(2,1)S(1)}, u32[]{:S(2)}, u32[]{:S(2)}) collective-permute-start(bf16[48,48,8]{1,2,0:T(8,128)(2,1)S(1)} %copy.96), channel_id=1, source_target_pairs={{1,0},{2,1},{3,2},{4,3},{5,4},{6,5},{7,6},{9,8},{10,9},{11,10},{12... | collective-permute-start | bytes 110600 | tf_op jit(solution)/shard_map/ppermute | solution.py:17
Sparse Core Ops, SparseCore 0:
  204.6 248.4 all-reduce.1
where the time goes:
time: 492 us; the launch traced here: 491 us
  waiting for transfers between devices  276 us (56%)
  starting transfers between devices  73.8 us (15%)
  blocking collectives  73.6 us (15%)
  local copies, waits for them, and re-layouts  32.3 us (7%)
  between operations  14.7 us (3%)
  matrix products  11.8 us (2%)
  other arithmetic  8.4 us (2%)
    psum x1, waiting for transfers between devices, shards(): lax.psum((local_kernel, local_mixing), ('row', 'col'))  240 us
    psum x1, blocking collectives, shards(): lax.psum((local_kernel, local_mixing), ('row', 'col'))  73.6 us
    all_to_all x2, waiting for transfers between devices, mirror_tile(): lax.all_to_all(strip, 'row', split_axis=2, concat_axis=1, tiled=True)  22.2 us
    unnamed x39, local copies, waits for them, and re-layouts  20.5 us
    ppermute x4, starting transfers between devices, with_halo(): after = lax.ppermute(initial, axis, down)  18.4 us
    all_to_all x2, starting transfers between devices, mirror_tile(): strip = lax.all_to_all(tile, 'col', split_axis=1, concat_axis=2, tiled=True)  15.6 us
    ppermute x4, starting transfers between devices, with_halo(): before = lax.ppermute(last, axis, up)  14.4 us
    all_to_all x2, starting transfers between devices, mirror_tile(): lax.all_to_all(turned, 'col', split_axis=2, concat_axis=3, tiled=True)  12.7 us
  transfers between devices with their start and end apart: 15, of which 7 were waited for; matrix products, arithmetic and copies ran while one was open for 8% of the time, Pallas kernels for 0%

commit v1 on v0

--- a/solution.py
+++ b/solution.py
@@ -17,6 +17,19 @@
         after = lax.ppermute(initial, axis, down)
         array = jnp.concatenate([before, array, after], axis=dim)
     return array
+
+
+def all_sum(x, axes):
+    for axis in axes:
+        peers = lax.axis_size(axis)
+        if peers & (peers - 1):
+            x = lax.psum(x, axis)
+            continue
+        step = 1
+        while step < peers:
+            x = x + lax.ppermute(x, axis, [(i, i ^ step) for i in range(peers)])
+            step *= 2
+    return x
 
 
 def mirror_tile(tile):
@@ -70,7 +83,8 @@
                 jnp.einsum("ihw,ohw->io", piece, grad_before, preferred_element_type=jnp.float32)
             )
     local_kernel = jnp.stack(tap_grads).reshape(3, 3, chans, chans)
-    grad_kernel, grad_mixing = lax.psum((local_kernel, local_mixing), ("row", "col"))
+    sums = all_sum(jnp.concatenate([local_kernel.reshape(9, chans, chans), local_mixing[None]]), ("row", "col"))
+    grad_kernel, grad_mixing = sums[:9].reshape(3, 3, chans, chans), sums[9]
     grad_padded = with_halo(grad_before, (("row", 1), ("col", 2)), DILATION)
     grad_active = jnp.zeros((chans, rows, cols), jnp.float32)
     for row_tap in range(3):

time: 492 us -> 224 us (0.46)
  waiting for transfers between devices: 276 us -> 55.9 us
  blocking collectives: 73.6 us -> 0 us
  starting transfers between devices: 73.8 us -> 89.2 us
  between operations: 14.7 us -> 1.26 us
  matrix products: 11.8 us -> 24.2 us
  local copies, waits for them, and re-layouts: 32.3 us -> 40.5 us
    psum x1 -> x0, waiting for transfers between devices: 240 us -> none  [shards(): lax.psum((local_kernel, local_mixing), ('row', 'col'))]
    psum x1 -> x0, blocking collectives: 73.6 us -> none  [shards(): lax.psum((local_kernel, local_mixing), ('row', 'col'))]
    ppermute x0 -> x8, waiting for transfers between devices: none -> 35.6 us  [all_sum(): x = x + lax.ppermute(x, axis, [(i, i ^ step) for i in range(peers)])]
    ppermute x0 -> x8, starting transfers between devices: none -> 14.1 us  [all_sum(): x = x + lax.ppermute(x, axis, [(i, i ^ step) for i in range(peers)])]
    all_to_all x2, waiting for transfers between devices: 22.2 us -> 9.68 us  [mirror_tile(): lax.all_to_all(strip, 'row', split_axis=2, concat_axis=1, tiled=True)]
    unnamed x39 -> x43, local copies, waits for them, and re-layouts: 20.5 us -> 22.8 us
  transfers between devices with their start and end apart: 15 -> 22, of which waited for: 7 -> 11; matrix products, arithmetic and copies ran while one was open for 8% -> 30% of each run, Pallas kernels for 0% -> 0%
where the time goes in v1:
time: 224 us; the launch traced here: 222 us
  starting transfers between devices  89.2 us (40%)
  waiting for transfers between devices  55.9 us (25%)
  local copies, waits for them, and re-layouts  40.5 us (18%)
  matrix products  24.2 us (11%)
  other arithmetic  11.4 us (5%)
    ppermute x8, waiting for transfers between devices, all_sum(): x = x + lax.ppermute(x, axis, [(i, i ^ step) for i in range(peers)])  35.6 us
    unnamed x43, local copies, waits for them, and re-layouts  22.8 us
    ppermute x4, starting transfers between devices, with_halo(): after = lax.ppermute(initial, axis, down)  19.7 us
    all_to_all x2, starting transfers between devices, mirror_tile(): strip = lax.all_to_all(tile, 'col', split_axis=1, concat_axis=2, tiled=True)  15.6 us
    ppermute x8, starting transfers between devices, all_sum(): x = x + lax.ppermute(x, axis, [(i, i ^ step) for i in range(peers)])  14.1 us
    ppermute x4, starting transfers between devices, with_halo(): before = lax.ppermute(last, axis, up)  13.6 us
    all_to_all x2, starting transfers between devices, mirror_tile(): lax.all_to_all(turned, 'col', split_axis=2, concat_axis=3, tiled=True)  13.3 us
    all_to_all x2, starting transfers between devices, mirror_tile(): lax.all_to_all(strip, 'row', split_axis=2, concat_axis=1, tiled=True)  12.8 us
  transfers between devices with their start and end apart: 22, of which 11 were waited for; matrix products, arithmetic and copies ran while one was open for 30% of the time, Pallas kernels for 0%

profile of v1, /device:TPU:6, one launch (start us, length us, event | category | flops | bytes accessed | tf_op | source)
XLA Modules:
  0.0 222.4 jit_solution(2431543495143858712)
XLA Ops:
  0.7 1.2 copy_maximum_fusion
  1.9 1.9 collective-permute-start
  3.8 7.5 %collective-permute-start.1 = (bf16[48,8,128]{2,0,1:T(8,128)(2,1)S(1)}, bf16[48,8,128]{2,0,1:T(8,128)(2,1)S(1)}, u32[]{:S(2)}, u32[]{:S(2)}) collective-permute-start(bf16[48,8,128]{2,0,1:T(8,128)(2,1)S(1)} %get-tuple-element.27), channel_id=1, source_target_pairs={{8,0},{16,8},{24,16},{32,24},{40,32},{48,40},{56,48},{64,56},{72,6... | collective-permute-start | bytes 294920 | tf_op jit(solution)/shard_map/ppermute | solution.py:17
  12.2 7.4 %all-to-all-start.3 = ((bf16[48,32,128]{2,0,1:T(8,128)(2,1)}), bf16[48,32,128]{2,0,1:T(8,128)(2,1)}, u32[]{:S(2)}, u32[]{:S(2)}) async-start(bf16[48,32,128]{2,0,1:T(8,128)(2,1)} %copy.88), calls=%async_computation.3 | async-start | bytes 786432 | tf_op jit(solution)/shard_map/all_to_all | solution.py:40
  21.6 1.9 collective-permute-start.3
  23.6 6.3 %collective-permute-start.2 = (bf16[48,48,8]{1,2,0:T(8,128)(2,1)S(1)}, bf16[48,48,8]{1,2,0:T(8,128)(2,1)S(1)}, u32[]{:S(2)}, u32[]{:S(2)}) collective-permute-start(bf16[48,48,8]{1,2,0:T(8,128)(2,1)S(1)} %copy.68), channel_id=1, source_target_pairs={{0,1},{1,2},{2,3},{3,4},{4,5},{5,6},{6,7},{8,9},{9,10},{10,11},{11... | collective-permute-start | bytes 110600 | tf_op jit(solution)/shard_map/ppermute | solution.py:16
  29.9 1.0 fusion.49
  30.9 1.2 collective-permute-done.2
  33.1 1.8 maximum_maximum_fusion
  37.7 1.6 copy.91
  39.3 2.5 %reshape.67 = bf16[32,2,3072]{2,1,0:T(2,128)(2,1)} reshape(bf16[1024,4,48]{2,1,0:T(4,128)(2,1)S(1)} %bitcast.228) | data formatting | bytes 786432
  41.7 7.6 %all-to-all-start.4 = ((bf16[32,2,3072]{2,1,0:T(2,128)(2,1)}), bf16[32,2,3072]{2,1,0:T(2,128)(2,1)S(1)}, u32[]{:S(2)}, u32[]{:S(2)}) async-start(bf16[32,2,3072]{2,1,0:T(2,128)(2,1)} %reshape.67), calls=%async_computation.4 | async-start | bytes 786432 | tf_op jit(solution)/shard_map/all_to_all | solution.py:41
  49.4 1.0 fusion.54
  50.4 1.8 fusion.11
  52.2 2.0 fusion.12
  54.2 9.7 %all-to-all-done.4 = bf16[32,2,3072]{2,1,0:T(2,128)(2,1)S(1)} async-done(((bf16[32,2,3072]{2,1,0:T(2,128)(2,1)}), bf16[32,2,3072]{2,1,0:T(2,128)(2,1)S(1)}, u32[]{:S(2)}, u32[]{:S(2)}) %all-to-all-start.4) | async-done | bytes 393248 | tf_op jit(solution)/shard_map/all_to_all | solution.py:41
  63.9 8.1 %all-to-all-start = ((bf16[48,32,128]{2,0,1:T(8,128)(2,1)}), bf16[48,32,128]{2,0,1:T(8,128)(2,1)S(1)}, u32[]{:S(2)}, u32[]{:S(2)}) async-start(bf16[48,32,128]{2,0,1:T(8,128)(2,1)} %fusion.12), calls=%async_computation | async-start | bytes 786432 | tf_op jit(solution)/shard_map/all_to_all | solution.py:40
  72.0 1.1 reshape.68
  73.3 2.3 %reshape.69 = bf16[8,2,12288]{2,1,0:T(2,128)(2,1)} reshape(bf16[32,4,32,48]{3,2,1,0:T(8,128)(2,1)S(1)} %bitcast.230) | data formatting | bytes 786432
  75.6 3.2 %all-to-all-done = bf16[48,32,128]{2,0,1:T(8,128)(2,1)S(1)} async-done(((bf16[48,32,128]{2,0,1:T(8,128)(2,1)}), bf16[48,32,128]{2,0,1:T(8,128)(2,1)S(1)}, u32[]{:S(2)}, u32[]{:S(2)}) %all-to-all-start) | async-done | bytes 393248 | tf_op jit(solution)/shard_map/all_to_all | solution.py:40
  78.9 6.0 %all-to-all-start.5 = ((bf16[8,2,12288]{2,1,0:T(2,128)(2,1)}), bf16[8,2,12288]{2,1,0:T(2,128)(2,1)S(1)}, u32[]{:S(2)}, u32[]{:S(2)}) async-start(bf16[8,2,12288]{2,1,0:T(2,128)(2,1)} %reshape.69), calls=%async_computation.5 | async-start | bytes 786432 | tf_op jit(solution)/shard_map/all_to_all | solution.py:43
  85.6 2.5 %reshape.63 = bf16[32,2,3072]{2,1,0:T(2,128)(2,1)} reshape(bf16[1024,4,48]{2,1,0:T(4,128)(2,1)S(1)} %bitcast.231) | data formatting | bytes 786432
  88.0 3.7 %all-to-all-done.5 = bf16[8,2,12288]{2,1,0:T(2,128)(2,1)S(1)} async-done(((bf16[8,2,12288]{2,1,0:T(2,128)(2,1)}), bf16[8,2,12288]{2,1,0:T(2,128)(2,1)S(1)}, u32[]{:S(2)}, u32[]{:S(2)}) %all-to-all-start.5) | async-done | bytes 393248 | tf_op jit(solution)/shard_map/all_to_all | solution.py:43
  91.7 5.2 %all-to-all-start.1 = ((bf16[32,2,3072]{2,1,0:T(2,128)(2,1)}), bf16[32,2,3072]{2,1,0:T(2,128)(2,1)}, u32[]{:S(2)}, u32[]{:S(2)}) async-start(bf16[32,2,3072]{2,1,0:T(2,128)(2,1)} %reshape.63), calls=%async_computation.1 | async-start | bytes 786432 | tf_op jit(solution)/shard_map/all_to_all | solution.py:41
  96.9 1.1 reshape.70
  98.5 1.3 copy.95
  99.8 1.5 fusion.8
  102.9 2.0 collective-permute-start.4
  105.0 5.8 %collective-permute-start.5 = (bf16[48,8,128]{2,0,1:T(8,128)(2,1)}, bf16[48,8,128]{2,0,1:T(8,128)(2,1)}, u32[]{:S(2)}, u32[]{:S(2)}) collective-permute-start(bf16[48,8,128]{2,0,1:T(8,128)(2,1)} %get-tuple-element.25), channel_id=1, source_target_pairs={{8,0},{16,8},{24,16},{32,24},{40,32},{48,40},{56,48},{64,56},{72,6... | collective-permute-start | bytes 294920 | tf_op jit(solution)/shard_map/ppermute | solution.py:17
  111.6 0.9 fusion.21
  116.9 0.9 fusion.16
  117.8 2.0 fusion.15
  119.8 3.3 %reshape.64 = bf16[1024,4,48]{2,1,0:T(4,128)(2,1)S(1)} reshape(bf16[32,2,3072]{2,1,0:T(2,128)(2,1)} %all-to-all-done.1) | data formatting | bytes 786432
  123.1 1.2 copy.166
  124.3 3.7 %reshape.65 = bf16[8,2,12288]{2,1,0:T(2,128)(2,1)} reshape(bf16[32,4,32,48]{3,2,1,0:T(8,128)(2,1)} %bitcast.233) | data formatting | bytes 786432
  128.1 7.3 %all-to-all-start.2 = ((bf16[8,2,12288]{2,1,0:T(2,128)(2,1)}), bf16[8,2,12288]{2,1,0:T(2,128)(2,1)}, u32[]{:S(2)}, u32[]{:S(2)}) async-start(bf16[8,2,12288]{2,1,0:T(2,128)(2,1)} %reshape.65), calls=%async_computation.2 | async-start | bytes 786432 | tf_op jit(solution)/shard_map/all_to_all | solution.py:43
  135.4 1.0 add.118
  136.7 1.0 pad_maximum_fusion.3
  137.7 1.0 fusion.115
  138.7 2.2 copy.96
  141.4 3.4 %collective-permute-start.7 = (bf16[48,48,8]{1,2,0:T(8,128)(2,1)S(1)}, bf16[48,48,8]{1,2,0:T(8,128)(2,1)}, u32[]{:S(2)}, u32[]{:S(2)}) collective-permute-start(bf16[48,48,8]{1,2,0:T(8,128)(2,1)S(1)} %copy.100), channel_id=1, source_target_pairs={{0,1},{1,2},{2,3},{3,4},{4,5},{5,6},{6,7},{8,9},{9,10},{10,11},{11... | collective-permute-start | bytes 110600 | tf_op jit(solution)/shard_map/ppermute | solution.py:16
  144.8 4.6 %collective-permute-start.6 = (bf16[48,48,8]{1,2,0:T(8,128)(2,1)}, bf16[48,48,8]{1,2,0:T(8,128)(2,1)}, u32[]{:S(2)}, u32[]{:S(2)}) collective-permute-start(bf16[48,48,8]{1,2,0:T(8,128)(2,1)} %copy.96), channel_id=1, source_target_pairs={{1,0},{2,1},{3,2},{4,3},{5,4},{6,5},{7,6},{9,8},{10,9},{11,10},{12... | collective-permute-start | bytes 110600 | tf_op jit(solution)/shard_map/ppermute | solution.py:17
  149.4 1.1 fusion.31
  150.5 1.1 fusion.35
  151.7 2.4 %collective-permute-done.6 = bf16[48,48,8]{1,2,0:T(8,128)(2,1)} collective-permute-done((bf16[48,48,8]{1,2,0:T(8,128)(2,1)}, bf16[48,48,8]{1,2,0:T(8,128)(2,1)}, u32[]{:S(2)}, u32[]{:S(2)}) %collective-permute-start.6) | collective-permute-done | bytes 36896 | tf_op jit(solution)/shard_map/ppermute | solution.py:17
  154.0 2.1 copy.97
  156.2 2.2 copy.101
  158.4 2.1 pad_maximum_fusion.1
  161.5 2.9 %collective-permute-start.10 = (f32[10,48,48]{2,1,0:T(8,128)S(1)}, f32[10,48,48]{2,1,0:T(8,128)S(1)}, u32[]{:S(2)}, u32[]{:S(2)}) collective-permute-start(f32[10,48,48]{2,1,0:T(8,128)S(1)} %add.119), channel_id=1, source_target_pairs={{0,32},{8,40},{16,48},{24,56},{32,0},{40,8},{48,16},{56,24},{64,96... | collective-permute-start | bytes 276488 | tf_op jit(solution)/shard_map/ppermute | solution.py:30
  164.6 10.1 %collective-permute-done.10 = f32[10,48,48]{2,1,0:T(8,128)S(1)} collective-permute-done((f32[10,48,48]{2,1,0:T(8,128)S(1)}, f32[10,48,48]{2,1,0:T(8,128)S(1)}, u32[]{:S(2)}, u32[]{:S(2)}) %collective-permute-start.10) | collective-permute-done | bytes 92192 | tf_op jit(solution)/shard_map/ppermute | solution.py:30
  174.7 4.7 %collective-permute-start.11 = (f32[10,48,48]{2,1,0:T(8,128)S(1)}, f32[10,48,48]{2,1,0:T(8,128)S(1)}, u32[]{:S(2)}, u32[]{:S(2)}) collective-permute-start(f32[10,48,48]{2,1,0:T(8,128)S(1)} %add.120), channel_id=1, source_target_pairs={{0,64},{8,72},{16,80},{24,88},{32,96},{40,104},{48,112},{56,120},{... | collective-permute-start | bytes 276488 | tf_op jit(solution)/shard_map/ppermute | solution.py:30
  179.6 11.5 %collective-permute-done.11 = f32[10,48,48]{2,1,0:T(8,128)S(1)} collective-permute-done((f32[10,48,48]{2,1,0:T(8,128)S(1)}, f32[10,48,48]{2,1,0:T(8,128)S(1)}, u32[]{:S(2)}, u32[]{:S(2)}) %collective-permute-start.11) | collective-permute-done | bytes 92192 | tf_op jit(solution)/shard_map/ppermute | solution.py:30
  191.4 6.4 %collective-permute-done.12 = f32[10,48,48]{2,1,0:T(8,128)S(1)} collective-permute-done((f32[10,48,48]{2,1,0:T(8,128)S(1)}, f32[10,48,48]{2,1,0:T(8,128)S(1)}, u32[]{:S(2)}, u32[]{:S(2)}) %collective-permute-start.12) | collective-permute-done | bytes 92192 | tf_op jit(solution)/shard_map/ppermute | solution.py:30
  197.9 1.9 collective-permute-start.13
  199.7 1.3 fusion.9
  201.0 2.3 %reshape.66 = bf16[32,4,32,48]{3,2,1,0:T(8,128)(2,1)S(1)} reshape(bf16[8,2,12288]{2,1,0:T(2,128)(2,1)} %all-to-all-done.2) | data formatting | bytes 786432
  203.3 2.4 %collective-permute-done.13 = f32[10,48,48]{2,1,0:T(8,128)S(1)} collective-permute-done((f32[10,48,48]{2,1,0:T(8,128)S(1)}, f32[10,48,48]{2,1,0:T(8,128)S(1)}, u32[]{:S(2)}, u32[]{:S(2)}) %collective-permute-start.13) | collective-permute-done | bytes 92192 | tf_op jit(solution)/shard_map/ppermute | solution.py:30
  205.7 1.7 collective-permute-start.14
  207.9 1.3 copy.87
  209.3 3.0 %collective-permute-done.14 = f32[10,48,48]{2,1,0:T(8,128)} collective-permute-done((f32[10,48,48]{2,1,0:T(8,128)S(1)}, f32[10,48,48]{2,1,0:T(8,128)}, u32[]{:S(2)}, u32[]{:S(2)}) %collective-permute-start.14) | collective-permute-done | bytes 92192 | tf_op jit(solution)/shard_map/ppermute | solution.py:30
  212.3 1.0 add.124
  213.3 2.6 %collective-permute-start.15 = (f32[10,48,48]{2,1,0:T(8,128)S(1)}, f32[10,48,48]{2,1,0:T(8,128)S(1)}, u32[]{:S(2)}, u32[]{:S(2)}) collective-permute-start(f32[10,48,48]{2,1,0:T(8,128)S(1)} %add.124), channel_id=1, source_target_pairs={{0,4},{1,5},{2,6},{3,7},{4,0},{5,1},{6,2},{7,3},{8,12},{9,13},{10,... | collective-permute-start | bytes 276488 | tf_op jit(solution)/shard_map/ppermute | solution.py:30
  215.9 1.2 add_convert_fusion
  218.8 2.3 %collective-permute-done.15 = f32[10,48,48]{2,1,0:T(8,128)S(1)} collective-permute-done((f32[10,48,48]{2,1,0:T(8,128)S(1)}, f32[10,48,48]{2,1,0:T(8,128)S(1)}, u32[]{:S(2)}, u32[]{:S(2)}) %collective-permute-start.15) | collective-permute-done | bytes 92192 | tf_op jit(solution)/shard_map/ppermute | solution.py:30
  (91 shorter events, 20.9 us)
Async XLA Ops:
  0.6 51.5 %copy-start = (bf16[48,48]{1,0:T(8,128)(2,1)S(1)}, bf16[48,48]{1,0:T(8,128)(2,1)}, u32[]{:S(2)}) copy-start(bf16[48,48]{1,0:T(8,128)(2,1)} %param.6) | copy-start | bytes 13828
  0.6 10.6 %copy-start.1 = (bf16[48,32,128]{2,1,0:T(8,128)(2,1)S(1)}, bf16[48,32,128]{2,1,0:T(8,128)(2,1)}, u32[]{:S(2)}) copy-start(bf16[48,32,128]{2,1,0:T(8,128)(2,1)} %param.7) | copy-start | bytes 1179652
  1.9 17.8 %collective-permute-start = (bf16[48,8,128]{2,0,1:T(8,128)(2,1)S(1)}, bf16[48,8,128]{2,0,1:T(8,128)(2,1)S(1)}, u32[]{:S(2)}, u32[]{:S(2)}) collective-permute-start(bf16[48,8,128]{2,0,1:T(8,128)(2,1)S(1)} %get-tuple-element.26), channel_id=1, source_target_pairs={{0,8},{8,16},{16,24},{24,32},{32,40},{40,48},{48,56},{56,64},{64,7... | collective-permute-start | bytes 294920 | tf_op jit(solution)/shard_map/ppermute | solution.py:16
  3.8 15.8 %collective-permute-start.1 = (bf16[48,8,128]{2,0,1:T(8,128)(2,1)S(1)}, bf16[48,8,128]{2,0,1:T(8,128)(2,1)S(1)}, u32[]{:S(2)}, u32[]{:S(2)}) collective-permute-start(bf16[48,8,128]{2,0,1:T(8,128)(2,1)S(1)} %get-tuple-element.27), channel_id=1, source_target_pairs={{8,0},{16,8},{24,16},{32,24},{40,32},{48,40},{56,48},{64,56},{72,6... | collective-permute-start | bytes 294920 | tf_op jit(solution)/shard_map/ppermute | solution.py:17
  12.2 25.5 %all-to-all-start.3 = ((bf16[48,32,128]{2,0,1:T(8,128)(2,1)}), bf16[48,32,128]{2,0,1:T(8,128)(2,1)}, u32[]{:S(2)}, u32[]{:S(2)}) async-start(bf16[48,32,128]{2,0,1:T(8,128)(2,1)} %copy.88), calls=%async_computation.3 | async-start | bytes 786432 | tf_op jit(solution)/shard_map/all_to_all | solution.py:40
  19.6 11.3 %copy-start.12 = (bf16[48,8,128]{2,0,1:T(8,128)(2,1)}, bf16[48,8,128]{2,0,1:T(8,128)(2,1)S(1)}, u32[]{:S(2)}) copy-start(bf16[48,8,128]{2,0,1:T(8,128)(2,1)S(1)} %collective-permute-done) | copy-start | bytes 294916
  19.6 0.7 copy-start.10
  21.6 10.9 %collective-permute-start.3 = (bf16[48,48,8]{1,2,0:T(8,128)(2,1)S(1)}, bf16[48,48,8]{1,2,0:T(8,128)(2,1)S(1)}, u32[]{:S(2)}, u32[]{:S(2)}) collective-permute-start(bf16[48,48,8]{1,2,0:T(8,128)(2,1)S(1)} %copy.72), channel_id=1, source_target_pairs={{1,0},{2,1},{3,2},{4,3},{5,4},{6,5},{7,6},{9,8},{10,9},{11,10},{12... | collective-permute-start | bytes 110600 | tf_op jit(solution)/shard_map/ppermute | solution.py:17
  23.6 8.5 %collective-permute-start.2 = (bf16[48,48,8]{1,2,0:T(8,128)(2,1)S(1)}, bf16[48,48,8]{1,2,0:T(8,128)(2,1)S(1)}, u32[]{:S(2)}, u32[]{:S(2)}) collective-permute-start(bf16[48,48,8]{1,2,0:T(8,128)(2,1)S(1)} %copy.68), channel_id=1, source_target_pairs={{0,1},{1,2},{2,3},{3,4},{4,5},{5,6},{6,7},{8,9},{9,10},{10,11},{11... | collective-permute-start | bytes 110600 | tf_op jit(solution)/shard_map/ppermute | solution.py:16
  33.1 1.9 copy-start.14
  34.9 2.5 %copy-start.7 = (bf16[48,48,136]{2,0,1:T(8,128)(2,1)}, bf16[48,48,136]{2,0,1:T(8,128)(2,1)S(1)}, u32[]{:S(2)}) copy-start(bf16[48,48,136]{2,0,1:T(8,128)(2,1)S(1)} %get-tuple-element.20) | copy-start | bytes 1880068
  34.9 14.4 %copy-start.5 = (bf16[48,48,136]{2,0,1:T(8,128)(2,1)}, bf16[48,48,136]{2,0,1:T(8,128)(2,1)S(1)}, u32[]{:S(2)}) copy-start(bf16[48,48,136]{2,0,1:T(8,128)(2,1)S(1)} %get-tuple-element.21) | copy-start | bytes 1880068
  35.6 1.1 copy-start.3
  41.7 8.7 %copy-start.11 = (bf16[48,8,128]{2,0,1:T(8,128)(2,1)S(1)}, bf16[48,8,128]{2,0,1:T(8,128)(2,1)}, u32[]{:S(2)}) copy-start(bf16[48,8,128]{2,0,1:T(8,128)(2,1)} %copy-done.10) | copy-start | bytes 294916
  41.7 22.2 %all-to-all-start.4 = ((bf16[32,2,3072]{2,1,0:T(2,128)(2,1)}), bf16[32,2,3072]{2,1,0:T(2,128)(2,1)S(1)}, u32[]{:S(2)}, u32[]{:S(2)}) async-start(bf16[32,2,3072]{2,1,0:T(2,128)(2,1)} %reshape.67), calls=%async_computation.4 | async-start | bytes 786432 | tf_op jit(solution)/shard_map/all_to_all | solution.py:41
  63.9 15.0 %all-to-all-start = ((bf16[48,32,128]{2,0,1:T(8,128)(2,1)}), bf16[48,32,128]{2,0,1:T(8,128)(2,1)S(1)}, u32[]{:S(2)}, u32[]{:S(2)}) async-start(bf16[48,32,128]{2,0,1:T(8,128)(2,1)} %fusion.12), calls=%async_computation | async-start | bytes 786432 | tf_op jit(solution)/shard_map/all_to_all | solution.py:40
  78.9 12.9 %all-to-all-start.5 = ((bf16[8,2,12288]{2,1,0:T(2,128)(2,1)}), bf16[8,2,12288]{2,1,0:T(2,128)(2,1)S(1)}, u32[]{:S(2)}, u32[]{:S(2)}) async-start(bf16[8,2,12288]{2,1,0:T(2,128)(2,1)} %reshape.69), calls=%async_computation.5 | async-start | bytes 786432 | tf_op jit(solution)/shard_map/all_to_all | solution.py:43
  91.7 28.1 %all-to-all-start.1 = ((bf16[32,2,3072]{2,1,0:T(2,128)(2,1)}), bf16[32,2,3072]{2,1,0:T(2,128)(2,1)}, u32[]{:S(2)}, u32[]{:S(2)}) async-start(bf16[32,2,3072]{2,1,0:T(2,128)(2,1)} %reshape.63), calls=%async_computation.1 | async-start | bytes 786432 | tf_op jit(solution)/shard_map/all_to_all | solution.py:41
  99.8 2.3 %copy-start.8 = (bf16[48,48,136]{2,0,1:T(8,128)(2,1)S(1)}, bf16[48,48,136]{2,0,1:T(8,128)(2,1)}, u32[]{:S(2)}) copy-start(bf16[48,48,136]{2,0,1:T(8,128)(2,1)} %copy-done.7) | copy-start | bytes 1880068
  99.8 10.9 %copy-start.13 = (bf16[48,8,128]{2,0,1:T(8,128)(2,1)S(1)}, bf16[48,8,128]{2,0,1:T(8,128)(2,1)}, u32[]{:S(2)}) copy-start(bf16[48,8,128]{2,0,1:T(8,128)(2,1)} %copy-done.12) | copy-start | bytes 294916
  101.4 10.2 %copy-start.6 = (bf16[48,48,136]{2,0,1:T(8,128)(2,1)S(1)}, bf16[48,48,136]{2,0,1:T(8,128)(2,1)}, u32[]{:S(2)}) copy-start(bf16[48,48,136]{2,0,1:T(8,128)(2,1)} %copy-done.5) | copy-start | bytes 1880068
  102.9 33.7 %collective-permute-start.4 = (bf16[48,8,128]{2,0,1:T(8,128)(2,1)}, bf16[48,8,128]{2,0,1:T(8,128)(2,1)}, u32[]{:S(2)}, u32[]{:S(2)}) collective-permute-start(bf16[48,8,128]{2,0,1:T(8,128)(2,1)} %get-tuple-element.24), channel_id=1, source_target_pairs={{0,8},{8,16},{16,24},{24,32},{32,40},{40,48},{48,56},{56,64},{64,7... | collective-permute-start | bytes 294920 | tf_op jit(solution)/shard_map/ppermute | solution.py:16
  105.0 8.4 %copy-start.4 = (bf16[48,32,128]{2,1,0:T(8,128)(2,1)S(1)}, bf16[48,32,128]{2,1,0:T(8,128)(2,1)}, u32[]{:S(2)}) copy-start(bf16[48,32,128]{2,1,0:T(8,128)(2,1)} %param.4) | copy-start | bytes 1179652
  105.0 31.7 %collective-permute-start.5 = (bf16[48,8,128]{2,0,1:T(8,128)(2,1)}, bf16[48,8,128]{2,0,1:T(8,128)(2,1)}, u32[]{:S(2)}, u32[]{:S(2)}) collective-permute-start(bf16[48,8,128]{2,0,1:T(8,128)(2,1)} %get-tuple-element.25), channel_id=1, source_target_pairs={{8,0},{16,8},{24,16},{32,24},{40,32},{48,40},{56,48},{64,56},{72,6... | collective-permute-start | bytes 294920 | tf_op jit(solution)/shard_map/ppermute | solution.py:17
  116.0 1.8 copy-start.2
  119.8 15.6 %collective-permute-start.8 = (f32[10,48,48]{2,1,0:T(8,128)}, f32[10,48,48]{2,1,0:T(8,128)S(1)}, u32[]{:S(2)}, u32[]{:S(2)}) collective-permute-start(f32[10,48,48]{2,1,0:T(8,128)} %fusion.15), channel_id=1, source_target_pairs={{0,8},{8,0},{16,24},{24,16},{32,40},{40,32},{48,56},{56,48},{64,72... | collective-permute-start | bytes 276488 | tf_op jit(solution)/shard_map/ppermute | solution.py:30
  128.1 73.0 %all-to-all-start.2 = ((bf16[8,2,12288]{2,1,0:T(2,128)(2,1)}), bf16[8,2,12288]{2,1,0:T(2,128)(2,1)}, u32[]{:S(2)}, u32[]{:S(2)}) async-start(bf16[8,2,12288]{2,1,0:T(2,128)(2,1)} %reshape.65), calls=%async_computation.2 | async-start | bytes 786432 | tf_op jit(solution)/shard_map/all_to_all | solution.py:43
  136.3 25.1 %collective-permute-start.9 = (f32[10,48,48]{2,1,0:T(8,128)S(1)}, f32[10,48,48]{2,1,0:T(8,128)S(1)}, u32[]{:S(2)}, u32[]{:S(2)}) collective-permute-start(f32[10,48,48]{2,1,0:T(8,128)S(1)} %add.118), channel_id=1, source_target_pairs={{0,16},{8,24},{16,0},{24,8},{32,48},{40,56},{48,32},{56,40},{64,80... | collective-permute-start | bytes 276488 | tf_op jit(solution)/shard_map/ppermute | solution.py:30
  138.7 10.7 %copy-start.15 = (bf16[3,3,48,48]{3,2,1,0:T(8,128)(2,1)S(1)}, bf16[3,3,48,48]{3,2,1,0:T(8,128)(2,1)}, u32[]{:S(2)}) copy-start(bf16[3,3,48,48]{3,2,1,0:T(8,128)(2,1)} %param.5) | copy-start | bytes 124420
  141.4 14.8 %collective-permute-start.7 = (bf16[48,48,8]{1,2,0:T(8,128)(2,1)S(1)}, bf16[48,48,8]{1,2,0:T(8,128)(2,1)}, u32[]{:S(2)}, u32[]{:S(2)}) collective-permute-start(bf16[48,48,8]{1,2,0:T(8,128)(2,1)S(1)} %copy.100), channel_id=1, source_target_pairs={{0,1},{1,2},{2,3},{3,4},{4,5},{5,6},{6,7},{8,9},{9,10},{10,11},{11... | collective-permute-start | bytes 110600 | tf_op jit(solution)/shard_map/ppermute | solution.py:16
  144.8 9.3 %collective-permute-start.6 = (bf16[48,48,8]{1,2,0:T(8,128)(2,1)}, bf16[48,48,8]{1,2,0:T(8,128)(2,1)}, u32[]{:S(2)}, u32[]{:S(2)}) collective-permute-start(bf16[48,48,8]{1,2,0:T(8,128)(2,1)} %copy.96), channel_id=1, source_target_pairs={{1,0},{2,1},{3,2},{4,3},{5,4},{6,5},{7,6},{9,8},{10,9},{11,10},{12... | collective-permute-start | bytes 110600 | tf_op jit(solution)/shard_map/ppermute | solution.py:17
  161.5 13.2 %collective-permute-start.10 = (f32[10,48,48]{2,1,0:T(8,128)S(1)}, f32[10,48,48]{2,1,0:T(8,128)S(1)}, u32[]{:S(2)}, u32[]{:S(2)}) collective-permute-start(f32[10,48,48]{2,1,0:T(8,128)S(1)} %add.119), channel_id=1, source_target_pairs={{0,32},{8,40},{16,48},{24,56},{32,0},{40,8},{48,16},{56,24},{64,96... | collective-permute-start | bytes 276488 | tf_op jit(solution)/shard_map/ppermute | solution.py:30
  174.7 16.4 %collective-permute-start.11 = (f32[10,48,48]{2,1,0:T(8,128)S(1)}, f32[10,48,48]{2,1,0:T(8,128)S(1)}, u32[]{:S(2)}, u32[]{:S(2)}) collective-permute-start(f32[10,48,48]{2,1,0:T(8,128)S(1)} %add.120), channel_id=1, source_target_pairs={{0,64},{8,72},{16,80},{24,88},{32,96},{40,104},{48,112},{56,120},{... | collective-permute-start | bytes 276488 | tf_op jit(solution)/shard_map/ppermute | solution.py:30
  191.1 6.8 %collective-permute-start.12 = (f32[10,48,48]{2,1,0:T(8,128)S(1)}, f32[10,48,48]{2,1,0:T(8,128)S(1)}, u32[]{:S(2)}, u32[]{:S(2)}) collective-permute-start(f32[10,48,48]{2,1,0:T(8,128)S(1)} %add.121), channel_id=1, source_target_pairs={{0,128},{8,136},{16,144},{24,152},{32,160},{40,168},{48,176},{56,1... | collective-permute-start | bytes 276488 | tf_op jit(solution)/shard_map/ppermute | solution.py:30
  197.9 7.8 %collective-permute-start.13 = (f32[10,48,48]{2,1,0:T(8,128)S(1)}, f32[10,48,48]{2,1,0:T(8,128)S(1)}, u32[]{:S(2)}, u32[]{:S(2)}) collective-permute-start(f32[10,48,48]{2,1,0:T(8,128)S(1)} %add.122), channel_id=1, source_target_pairs={{0,1},{1,0},{2,3},{3,2},{4,5},{5,4},{6,7},{7,6},{8,9},{9,8},{10,11... | collective-permute-start | bytes 276488 | tf_op jit(solution)/shard_map/ppermute | solution.py:30
  205.7 6.6 %collective-permute-start.14 = (f32[10,48,48]{2,1,0:T(8,128)S(1)}, f32[10,48,48]{2,1,0:T(8,128)}, u32[]{:S(2)}, u32[]{:S(2)}) collective-permute-start(f32[10,48,48]{2,1,0:T(8,128)S(1)} %add.123), channel_id=1, source_target_pairs={{0,2},{1,3},{2,0},{3,1},{4,6},{5,7},{6,4},{7,5},{8,10},{9,11},{10,... | collective-permute-start | bytes 276488 | tf_op jit(solution)/shard_map/ppermute | solution.py:30
  209.2 7.8 %copy-start.9 = (bf16[48,32,128]{2,0,1:T(8,128)(2,1)S(1)}, bf16[48,32,128]{2,0,1:T(8,128)(2,1)}, u32[]{:S(2)}) copy-start(bf16[48,32,128]{2,0,1:T(8,128)(2,1)} %fusion.9) | copy-start | bytes 1179652
  213.3 7.8 %collective-permute-start.15 = (f32[10,48,48]{2,1,0:T(8,128)S(1)}, f32[10,48,48]{2,1,0:T(8,128)S(1)}, u32[]{:S(2)}, u32[]{:S(2)}) collective-permute-start(f32[10,48,48]{2,1,0:T(8,128)S(1)} %add.124), channel_id=1, source_target_pairs={{0,4},{1,5},{2,6},{3,7},{4,0},{5,1},{6,2},{7,3},{8,12},{9,13},{10,... | collective-permute-start | bytes 276488 | tf_op jit(solution)/shard_map/ppermute | solution.py:30

commit v2 on v1

--- a/solution.py
+++ b/solution.py
@@ -83,8 +83,10 @@
                 jnp.einsum("ihw,ohw->io", piece, grad_before, preferred_element_type=jnp.float32)
             )
     local_kernel = jnp.stack(tap_grads).reshape(3, 3, chans, chans)
-    sums = all_sum(jnp.concatenate([local_kernel.reshape(9, chans, chans), local_mixing[None]]), ("row", "col"))
-    grad_kernel, grad_mixing = sums[:9].reshape(3, 3, chans, chans), sums[9]
+    flat = jnp.concatenate([local_kernel.reshape(-1), local_mixing.reshape(-1)])
+    sums = all_sum(flat.reshape(-1, 128), ("row", "col")).reshape(-1)
+    grad_kernel = sums[: 9 * chans * chans].reshape(3, 3, chans, chans)
+    grad_mixing = sums[9 * chans * chans :].reshape(chans, chans)
     grad_padded = with_halo(grad_before, (("row", 1), ("col", 2)), DILATION)
     grad_active = jnp.zeros((chans, rows, cols), jnp.float32)
     for row_tap in range(3):

time: 224 us -> 197 us (0.88)
  matrix products: 24.2 us -> 11.8 us
  local copies, waits for them, and re-layouts: 40.5 us -> 34.8 us
  starting transfers between devices: 89.2 us -> 83.5 us
  other arithmetic: 11.4 us -> 7.84 us
    ppermute x8, waiting for transfers between devices: 35.6 us -> 18.6 us  [all_sum(): x = x + lax.ppermute(x, axis, [(i, i ^ step) for i in range(peers)])]
    all_to_all x2, waiting for transfers between devices: 9.68 us -> 22.2 us  [mirror_tile(): lax.all_to_all(strip, 'row', split_axis=2, concat_axis=1, tiled=True)]
    dot_general x9, matrix products: 7.87 us -> 3.45 us  [shards(): jnp.einsum('ihw,ohw->io', piece, grad_before, preferred_element_type=jnp....]
    ppermute x8, starting transfers between devices: 14.1 us -> 9.95 us  [all_sum(): x = x + lax.ppermute(x, axis, [(i, i ^ step) for i in range(peers)])]
    ppermute x4, waiting for transfers between devices: 2.39 us -> 6.27 us  [with_halo(): after = lax.ppermute(initial, axis, down)]
    unnamed x43 -> x37, local copies, waits for them, and re-layouts: 22.8 us -> 19.7 us
    dot_general x9, matrix products: 5.62 us -> 2.75 us  [shards(): jnp.einsum('io,ihw->ohw', kernel[row_tap, col_tap], piece, preferred_elem...]
    dot_general x9, matrix products: 5.17 us -> 2.66 us  [shards(): jnp.einsum('io,ohw->ihw', kernel[row_tap, col_tap], piece, preferred_elem...]
  transfers between devices with their start and end apart: 22 -> 22, of which waited for: 11 -> 13; matrix products, arithmetic and copies ran while one was open for 30% -> 25% of each run, Pallas kernels for 0% -> 0%
where the time goes in v2:
time: 197 us; the launch traced here: 195 us
  starting transfers between devices  83.5 us (42%)
  waiting for transfers between devices  55.9 us (28%)
  local copies, waits for them, and re-layouts  34.8 us (18%)
  matrix products  11.8 us (6%)
  other arithmetic  7.84 us (4%)
    all_to_all x2, waiting for transfers between devices, mirror_tile(): lax.all_to_all(strip, 'row', split_axis=2, concat_axis=1, tiled=True)  22.2 us
    unnamed x37, local copies, waits for them, and re-layouts  19.7 us
    ppermute x4, starting transfers between devices, with_halo(): after = lax.ppermute(initial, axis, down)  18.6 us
    ppermute x8, waiting for transfers between devices, all_sum(): x = x + lax.ppermute(x, axis, [(i, i ^ step) for i in range(peers)])  18.6 us
    all_to_all x2, starting transfers between devices, mirror_tile(): strip = lax.all_to_all(tile, 'col', split_axis=1, concat_axis=2, tiled=True)  15.6 us
    ppermute x4, starting transfers between devices, with_halo(): before = lax.ppermute(last, axis, up)  14 us
    all_to_all x2, starting transfers between devices, mirror_tile(): lax.all_to_all(turned, 'col', split_axis=2, concat_axis=3, tiled=True)  12.7 us
    all_to_all x2, starting transfers between devices, mirror_tile(): lax.all_to_all(strip, 'row', split_axis=2, concat_axis=1, tiled=True)  12.6 us
  transfers between devices with their start and end apart: 22, of which 13 were waited for; matrix products, arithmetic and copies ran while one was open for 25% of the time, Pallas kernels for 0%

profile of v2, /device:TPU:6, one launch (start us, length us, event | category | flops | bytes accessed | tf_op | source)
XLA Modules:
  0.0 195.3 jit_solution(590049043005023555)
XLA Ops:
  0.7 1.2 copy_maximum_fusion
  1.9 1.9 collective-permute-start
  3.8 7.5 %collective-permute-start.1 = (bf16[48,8,128]{2,0,1:T(8,128)(2,1)S(1)}, bf16[48,8,128]{2,0,1:T(8,128)(2,1)S(1)}, u32[]{:S(2)}, u32[]{:S(2)}) collective-permute-start(bf16[48,8,128]{2,0,1:T(8,128)(2,1)S(1)} %get-tuple-element.27), channel_id=1, source_target_pairs={{8,0},{16,8},{24,16},{32,24},{40,32},{48,40},{56,48},{64,56},{72,6... | collective-permute-start | bytes 294920 | tf_op jit(solution)/shard_map/ppermute | solution.py:17
  11.3 0.9 copy.88
  12.2 7.4 %all-to-all-start.3 = ((bf16[48,32,128]{2,0,1:T(8,128)(2,1)}), bf16[48,32,128]{2,0,1:T(8,128)(2,1)S(1)}, u32[]{:S(2)}, u32[]{:S(2)}) async-start(bf16[48,32,128]{2,0,1:T(8,128)(2,1)} %copy.88), calls=%async_computation.3 | async-start | bytes 786432 | tf_op jit(solution)/shard_map/all_to_all | solution.py:40
  21.0 1.9 collective-permute-start.3
  22.9 6.3 %collective-permute-start.2 = (bf16[48,48,8]{1,2,0:T(8,128)(2,1)S(1)}, bf16[48,48,8]{1,2,0:T(8,128)(2,1)S(1)}, u32[]{:S(2)}, u32[]{:S(2)}) collective-permute-start(bf16[48,48,8]{1,2,0:T(8,128)(2,1)S(1)} %copy.68), channel_id=1, source_target_pairs={{0,1},{1,2},{2,3},{3,4},{4,5},{5,6},{6,7},{8,9},{9,10},{10,11},{11... | collective-permute-start | bytes 110600 | tf_op jit(solution)/shard_map/ppermute | solution.py:16
  29.5 1.9 collective-permute-done.2
  32.4 0.8 maximum_maximum_fusion
  34.6 0.7 copy-done.3
  36.5 0.7 copy-done.5
  37.3 1.0 fusion.12
  38.3 8.2 %all-to-all-start = ((bf16[48,32,128]{2,0,1:T(8,128)(2,1)}), bf16[48,32,128]{2,0,1:T(8,128)(2,1)S(1)}, u32[]{:S(2)}, u32[]{:S(2)}) async-start(bf16[48,32,128]{2,0,1:T(8,128)(2,1)} %fusion.12), calls=%async_computation | async-start | bytes 786432 | tf_op jit(solution)/shard_map/all_to_all | solution.py:40
  46.5 0.7 copy.91
  47.2 2.5 %reshape.81 = bf16[32,2,3072]{2,1,0:T(2,128)(2,1)} reshape(bf16[1024,4,48]{2,1,0:T(4,128)(2,1)S(1)} %bitcast.228) | data formatting | bytes 786432
  49.6 3.7 %all-to-all-done = bf16[48,32,128]{2,0,1:T(8,128)(2,1)S(1)} async-done(((bf16[48,32,128]{2,0,1:T(8,128)(2,1)}), bf16[48,32,128]{2,0,1:T(8,128)(2,1)S(1)}, u32[]{:S(2)}, u32[]{:S(2)}) %all-to-all-start) | async-done | bytes 393248 | tf_op jit(solution)/shard_map/all_to_all | solution.py:40
  53.3 7.5 %all-to-all-start.4 = ((bf16[32,2,3072]{2,1,0:T(2,128)(2,1)}), bf16[32,2,3072]{2,1,0:T(2,128)(2,1)S(1)}, u32[]{:S(2)}, u32[]{:S(2)}) async-start(bf16[32,2,3072]{2,1,0:T(2,128)(2,1)} %reshape.81), calls=%async_computation.4 | async-start | bytes 786432 | tf_op jit(solution)/shard_map/all_to_all | solution.py:41
  60.8 0.7 copy.122
  61.5 2.5 %reshape.77 = bf16[32,2,3072]{2,1,0:T(2,128)(2,1)} reshape(bf16[1024,4,48]{2,1,0:T(4,128)(2,1)S(1)} %bitcast.229) | data formatting | bytes 786432
  63.9 11.4 %all-to-all-done.4 = bf16[32,2,3072]{2,1,0:T(2,128)(2,1)S(1)} async-done(((bf16[32,2,3072]{2,1,0:T(2,128)(2,1)}), bf16[32,2,3072]{2,1,0:T(2,128)(2,1)S(1)}, u32[]{:S(2)}, u32[]{:S(2)}) %all-to-all-start.4) | async-done | bytes 393248 | tf_op jit(solution)/shard_map/all_to_all | solution.py:41
  75.3 5.2 %all-to-all-start.1 = ((bf16[32,2,3072]{2,1,0:T(2,128)(2,1)}), bf16[32,2,3072]{2,1,0:T(2,128)(2,1)S(1)}, u32[]{:S(2)}, u32[]{:S(2)}) async-start(bf16[32,2,3072]{2,1,0:T(2,128)(2,1)} %reshape.77), calls=%async_computation.1 | async-start | bytes 786432 | tf_op jit(solution)/shard_map/all_to_all | solution.py:41
  80.5 1.1 reshape.82
  81.8 2.3 %reshape.83 = bf16[8,2,12288]{2,1,0:T(2,128)(2,1)} reshape(bf16[32,4,32,48]{3,2,1,0:T(8,128)(2,1)S(1)} %bitcast.231) | data formatting | bytes 786432
  84.1 10.8 %all-to-all-done.1 = bf16[32,2,3072]{2,1,0:T(2,128)(2,1)S(1)} async-done(((bf16[32,2,3072]{2,1,0:T(2,128)(2,1)}), bf16[32,2,3072]{2,1,0:T(2,128)(2,1)S(1)}, u32[]{:S(2)}, u32[]{:S(2)}) %all-to-all-start.1) | async-done | bytes 393248 | tf_op jit(solution)/shard_map/all_to_all | solution.py:41
  94.9 6.0 %all-to-all-start.5 = ((bf16[8,2,12288]{2,1,0:T(2,128)(2,1)}), bf16[8,2,12288]{2,1,0:T(2,128)(2,1)S(1)}, u32[]{:S(2)}, u32[]{:S(2)}) async-start(bf16[8,2,12288]{2,1,0:T(2,128)(2,1)} %reshape.83), calls=%async_computation.5 | async-start | bytes 786432 | tf_op jit(solution)/shard_map/all_to_all | solution.py:43
  100.9 1.1 reshape.78
  102.2 2.3 %reshape.79 = bf16[8,2,12288]{2,1,0:T(2,128)(2,1)} reshape(bf16[32,4,32,48]{3,2,1,0:T(8,128)(2,1)S(1)} %bitcast.233) | data formatting | bytes 786432
  104.5 3.3 %all-to-all-done.5 = bf16[8,2,12288]{2,1,0:T(2,128)(2,1)S(1)} async-done(((bf16[8,2,12288]{2,1,0:T(2,128)(2,1)}), bf16[8,2,12288]{2,1,0:T(2,128)(2,1)S(1)}, u32[]{:S(2)}, u32[]{:S(2)}) %all-to-all-start.5) | async-done | bytes 393248 | tf_op jit(solution)/shard_map/all_to_all | solution.py:43
  107.8 6.7 %all-to-all-start.2 = ((bf16[8,2,12288]{2,1,0:T(2,128)(2,1)}), bf16[8,2,12288]{2,1,0:T(2,128)(2,1)}, u32[]{:S(2)}, u32[]{:S(2)}) async-start(bf16[8,2,12288]{2,1,0:T(2,128)(2,1)} %reshape.79), calls=%async_computation.2 | async-start | bytes 786432 | tf_op jit(solution)/shard_map/all_to_all | solution.py:43
  114.4 1.1 reshape.84
  116.0 1.3 copy.95
  117.3 1.6 convolution_bitcast_fusion.3
  119.4 1.3 fusion.21
  121.3 0.7 copy-done.10
  123.9 2.4 %collective-permute-start.4 = (bf16[48,8,128]{2,0,1:T(8,128)(2,1)S(1)}, bf16[48,8,128]{2,0,1:T(8,128)(2,1)S(1)}, u32[]{:S(2)}, u32[]{:S(2)}) collective-permute-start(bf16[48,8,128]{2,0,1:T(8,128)(2,1)S(1)} %get-tuple-element.24), channel_id=1, source_target_pairs={{0,8},{8,16},{16,24},{24,32},{32,40},{40,48},{48,56},{56,64},{64,7... | collective-permute-start | bytes 294920 | tf_op jit(solution)/shard_map/ppermute | solution.py:16
  126.3 5.3 %collective-permute-start.5 = (bf16[48,8,128]{2,0,1:T(8,128)(2,1)S(1)}, bf16[48,8,128]{2,0,1:T(8,128)(2,1)S(1)}, u32[]{:S(2)}, u32[]{:S(2)}) collective-permute-start(bf16[48,8,128]{2,0,1:T(8,128)(2,1)S(1)} %get-tuple-element.25), channel_id=1, source_target_pairs={{8,0},{16,8},{24,16},{32,24},{40,32},{48,40},{56,48},{64,56},{72,6... | collective-permute-start | bytes 294920 | tf_op jit(solution)/shard_map/ppermute | solution.py:17
  131.6 0.7 fusion.131
  132.3 1.5 collective-permute-done.5
  134.1 1.2 copy.96
  135.8 3.4 %collective-permute-start.7 = (bf16[48,48,8]{1,2,0:T(8,128)(2,1)S(1)}, bf16[48,48,8]{1,2,0:T(8,128)(2,1)S(1)}, u32[]{:S(2)}, u32[]{:S(2)}) collective-permute-start(bf16[48,48,8]{1,2,0:T(8,128)(2,1)S(1)} %copy.100), channel_id=1, source_target_pairs={{0,1},{1,2},{2,3},{3,4},{4,5},{5,6},{6,7},{8,9},{9,10},{10,11},{11... | collective-permute-start | bytes 110600 | tf_op jit(solution)/shard_map/ppermute | solution.py:16
  139.2 4.0 %collective-permute-start.6 = (bf16[48,48,8]{1,2,0:T(8,128)(2,1)}, bf16[48,48,8]{1,2,0:T(8,128)(2,1)}, u32[]{:S(2)}, u32[]{:S(2)}) collective-permute-start(bf16[48,48,8]{1,2,0:T(8,128)(2,1)} %copy.96), channel_id=1, source_target_pairs={{1,0},{2,1},{3,2},{4,3},{5,4},{6,5},{7,6},{9,8},{10,9},{11,10},{12... | collective-permute-start | bytes 110600 | tf_op jit(solution)/shard_map/ppermute | solution.py:17
  143.6 4.8 %collective-permute-done.6 = bf16[48,48,8]{1,2,0:T(8,128)(2,1)} collective-permute-done((bf16[48,48,8]{1,2,0:T(8,128)(2,1)}, bf16[48,48,8]{1,2,0:T(8,128)(2,1)}, u32[]{:S(2)}, u32[]{:S(2)}) %collective-permute-start.6) | collective-permute-done | bytes 36896 | tf_op jit(solution)/shard_map/ppermute | solution.py:17
  148.4 2.2 %copy.97 = bf16[48,48,8]{2,0,1:T(8,128)(2,1)} copy(bf16[48,48,8]{1,2,0:T(8,128)(2,1)} %collective-permute-done.6) | data formatting | bytes 73728 | tf_op jit(solution)/shard_map/ppermute | solution.py:17
  150.5 1.3 copy.101
  151.8 2.0 %pad_maximum_fusion.1 = (bf16[48,48,136]{2,0,1:T(8,128)(2,1)S(1)}, bf16[48,48,136]{2,0,1:T(8,128)(2,1)S(1)}) fusion(bf16[48,48,8]{2,0,1:T(8,128)(2,1)} %copy.97, bf16[48,8,128]{2,0,1:T(8,128)(2,1)S(1)} %collective-permute-done.5, bf16[48,32,128]{2,0,1:T(8,128)(2,1)S(1)} %fusion.8, bf16[48,8,128]{2,0,1:T(8,128)(2,1)S(1)} %collective-permute-done.4, ...), kind=kLoop, calls=%fused_computation.32 | loop fusion | flops 5013504 | bytes 1916928 | tf_op jit(solution)/shard_map/concatenate | solution.py:18
  154.8 0.9 fusion.132
  156.0 6.2 %collective-permute-done.10 = f32[180,128]{1,0:T(8,128)S(1)} collective-permute-done((f32[180,128]{1,0:T(8,128)S(1)}, f32[180,128]{1,0:T(8,128)S(1)}, u32[]{:S(2)}, u32[]{:S(2)}) %collective-permute-start.10) | collective-permute-done | bytes 92192 | tf_op jit(solution)/shard_map/ppermute | solution.py:30
  162.2 2.8 %collective-permute-start.11 = (f32[180,128]{1,0:T(8,128)S(1)}, f32[180,128]{1,0:T(8,128)S(1)}, u32[]{:S(2)}, u32[]{:S(2)}) collective-permute-start(f32[180,128]{1,0:T(8,128)S(1)} %add.120), channel_id=1, source_target_pairs={{0,64},{8,72},{16,80},{24,88},{32,96},{40,104},{48,112},{56,120},{... | collective-permute-start | bytes 276488 | tf_op jit(solution)/shard_map/ppermute | solution.py:30
  165.2 5.9 %collective-permute-done.11 = f32[180,128]{1,0:T(8,128)S(1)} collective-permute-done((f32[180,128]{1,0:T(8,128)S(1)}, f32[180,128]{1,0:T(8,128)S(1)}, u32[]{:S(2)}, u32[]{:S(2)}) %collective-permute-start.11) | collective-permute-done | bytes 92192 | tf_op jit(solution)/shard_map/ppermute | solution.py:30
  171.1 1.3 collective-permute-start.12
  172.7 3.1 %collective-permute-done.12 = f32[180,128]{1,0:T(8,128)S(1)} collective-permute-done((f32[180,128]{1,0:T(8,128)S(1)}, f32[180,128]{1,0:T(8,128)S(1)}, u32[]{:S(2)}, u32[]{:S(2)}) %collective-permute-start.12) | collective-permute-done | bytes 92192 | tf_op jit(solution)/shard_map/ppermute | solution.py:30
  175.8 1.3 collective-permute-start.13
  177.0 0.6 fusion.9
  177.6 2.3 %reshape.80 = bf16[32,4,32,48]{3,2,1,0:T(8,128)(2,1)S(1)} reshape(bf16[8,2,12288]{2,1,0:T(2,128)(2,1)} %all-to-all-done.2) | data formatting | bytes 786432
  179.9 2.0 %collective-permute-done.13 = f32[180,128]{1,0:T(8,128)S(1)} collective-permute-done((f32[180,128]{1,0:T(8,128)S(1)}, f32[180,128]{1,0:T(8,128)S(1)}, u32[]{:S(2)}, u32[]{:S(2)}) %collective-permute-start.13) | collective-permute-done | bytes 92192 | tf_op jit(solution)/shard_map/ppermute | solution.py:30
  182.0 1.6 collective-permute-start.14
  184.1 2.2 %copy.87 = f32[48,32,128]{2,0,1:T(8,128)} copy(f32[48,32,128]{0,1,2:T(8,128)S(1)} %bitcast.225) | data formatting | bytes 1572864 | tf_op jit(solution)/shard_map/convert_element_type | solution.py:71
  186.2 1.3 collective-permute-done.14
  187.5 2.9 %collective-permute-start.15 = (f32[180,128]{1,0:T(8,128)S(1)}, f32[180,128]{1,0:T(8,128)S(1)}, u32[]{:S(2)}, u32[]{:S(2)}) collective-permute-start(f32[180,128]{1,0:T(8,128)S(1)} %add.124), channel_id=1, source_target_pairs={{0,4},{1,5},{2,6},{3,7},{4,0},{5,1},{6,2},{7,3},{8,12},{9,13},{10,... | collective-permute-start | bytes 276488 | tf_op jit(solution)/shard_map/ppermute | solution.py:30
  190.4 1.5 add_convert_fusion
  191.9 0.8 copy.110
  192.7 0.8 copy.109
  193.7 0.7 div.21
  194.4 0.8 div.18
  (90 shorter events, 12.7 us)
Async XLA Ops:
  0.6 36.6 %copy-start = (bf16[48,48]{1,0:T(8,128)(2,1)S(1)}, bf16[48,48]{1,0:T(8,128)(2,1)}, u32[]{:S(2)}) copy-start(bf16[48,48]{1,0:T(8,128)(2,1)} %param.6) | copy-start | bytes 13828
  0.6 10.6 %copy-start.1 = (bf16[48,32,128]{2,1,0:T(8,128)(2,1)S(1)}, bf16[48,32,128]{2,1,0:T(8,128)(2,1)}, u32[]{:S(2)}) copy-start(bf16[48,32,128]{2,1,0:T(8,128)(2,1)} %param.7) | copy-start | bytes 1179652
  1.9 17.8 %collective-permute-start = (bf16[48,8,128]{2,0,1:T(8,128)(2,1)S(1)}, bf16[48,8,128]{2,0,1:T(8,128)(2,1)S(1)}, u32[]{:S(2)}, u32[]{:S(2)}) collective-permute-start(bf16[48,8,128]{2,0,1:T(8,128)(2,1)S(1)} %get-tuple-element.26), channel_id=1, source_target_pairs={{0,8},{8,16},{16,24},{24,32},{32,40},{40,48},{48,56},{56,64},{64,7... | collective-permute-start | bytes 294920 | tf_op jit(solution)/shard_map/ppermute | solution.py:16
  3.8 15.8 %collective-permute-start.1 = (bf16[48,8,128]{2,0,1:T(8,128)(2,1)S(1)}, bf16[48,8,128]{2,0,1:T(8,128)(2,1)S(1)}, u32[]{:S(2)}, u32[]{:S(2)}) collective-permute-start(bf16[48,8,128]{2,0,1:T(8,128)(2,1)S(1)} %get-tuple-element.27), channel_id=1, source_target_pairs={{8,0},{16,8},{24,16},{32,24},{40,32},{48,40},{56,48},{64,56},{72,6... | collective-permute-start | bytes 294920 | tf_op jit(solution)/shard_map/ppermute | solution.py:17
  12.2 26.1 %all-to-all-start.3 = ((bf16[48,32,128]{2,0,1:T(8,128)(2,1)}), bf16[48,32,128]{2,0,1:T(8,128)(2,1)S(1)}, u32[]{:S(2)}, u32[]{:S(2)}) async-start(bf16[48,32,128]{2,0,1:T(8,128)(2,1)} %copy.88), calls=%async_computation.3 | async-start | bytes 786432 | tf_op jit(solution)/shard_map/all_to_all | solution.py:40
  19.9 9.3 %copy-start.11 = (bf16[3,3,48,48]{3,2,1,0:T(8,128)(2,1)S(1)}, bf16[3,3,48,48]{3,2,1,0:T(8,128)(2,1)}, u32[]{:S(2)}) copy-start(bf16[3,3,48,48]{3,2,1,0:T(8,128)(2,1)} %param.5) | copy-start | bytes 124420
  21.0 10.9 %collective-permute-start.3 = (bf16[48,48,8]{1,2,0:T(8,128)(2,1)S(1)}, bf16[48,48,8]{1,2,0:T(8,128)(2,1)S(1)}, u32[]{:S(2)}, u32[]{:S(2)}) collective-permute-start(bf16[48,48,8]{1,2,0:T(8,128)(2,1)S(1)} %copy.72), channel_id=1, source_target_pairs={{1,0},{2,1},{3,2},{4,3},{5,4},{6,5},{7,6},{9,8},{10,9},{11,10},{12... | collective-permute-start | bytes 110600 | tf_op jit(solution)/shard_map/ppermute | solution.py:17
  22.9 8.5 %collective-permute-start.2 = (bf16[48,48,8]{1,2,0:T(8,128)(2,1)S(1)}, bf16[48,48,8]{1,2,0:T(8,128)(2,1)S(1)}, u32[]{:S(2)}, u32[]{:S(2)}) collective-permute-start(bf16[48,48,8]{1,2,0:T(8,128)(2,1)S(1)} %copy.68), channel_id=1, source_target_pairs={{0,1},{1,2},{2,3},{3,4},{4,5},{5,6},{6,7},{8,9},{9,10},{10,11},{11... | collective-permute-start | bytes 110600 | tf_op jit(solution)/shard_map/ppermute | solution.py:16
  33.3 2.3 %copy-start.7 = (bf16[48,48,136]{2,0,1:T(8,128)(2,1)}, bf16[48,48,136]{2,0,1:T(8,128)(2,1)S(1)}, u32[]{:S(2)}) copy-start(bf16[48,48,136]{2,0,1:T(8,128)(2,1)S(1)} %get-tuple-element.21) | copy-start | bytes 1880068
  33.3 2.6 %copy-start.9 = (bf16[48,48,136]{2,0,1:T(8,128)(2,1)}, bf16[48,48,136]{2,0,1:T(8,128)(2,1)S(1)}, u32[]{:S(2)}) copy-start(bf16[48,48,136]{2,0,1:T(8,128)(2,1)S(1)} %get-tuple-element.20) | copy-start | bytes 1880068
  34.3 1.0 copy-start.3
  36.5 0.8 copy-start.5
  38.3 15.0 %all-to-all-start = ((bf16[48,32,128]{2,0,1:T(8,128)(2,1)}), bf16[48,32,128]{2,0,1:T(8,128)(2,1)S(1)}, u32[]{:S(2)}, u32[]{:S(2)}) async-start(bf16[48,32,128]{2,0,1:T(8,128)(2,1)} %fusion.12), calls=%async_computation | async-start | bytes 786432 | tf_op jit(solution)/shard_map/all_to_all | solution.py:40
  53.3 22.0 %all-to-all-start.4 = ((bf16[32,2,3072]{2,1,0:T(2,128)(2,1)}), bf16[32,2,3072]{2,1,0:T(2,128)(2,1)S(1)}, u32[]{:S(2)}, u32[]{:S(2)}) async-start(bf16[32,2,3072]{2,1,0:T(2,128)(2,1)} %reshape.81), calls=%async_computation.4 | async-start | bytes 786432 | tf_op jit(solution)/shard_map/all_to_all | solution.py:41
  75.3 19.6 %all-to-all-start.1 = ((bf16[32,2,3072]{2,1,0:T(2,128)(2,1)}), bf16[32,2,3072]{2,1,0:T(2,128)(2,1)S(1)}, u32[]{:S(2)}, u32[]{:S(2)}) async-start(bf16[32,2,3072]{2,1,0:T(2,128)(2,1)} %reshape.77), calls=%async_computation.1 | async-start | bytes 786432 | tf_op jit(solution)/shard_map/all_to_all | solution.py:41
  94.9 12.9 %all-to-all-start.5 = ((bf16[8,2,12288]{2,1,0:T(2,128)(2,1)}), bf16[8,2,12288]{2,1,0:T(2,128)(2,1)S(1)}, u32[]{:S(2)}, u32[]{:S(2)}) async-start(bf16[8,2,12288]{2,1,0:T(2,128)(2,1)} %reshape.83), calls=%async_computation.5 | async-start | bytes 786432 | tf_op jit(solution)/shard_map/all_to_all | solution.py:43
  107.8 69.8 %all-to-all-start.2 = ((bf16[8,2,12288]{2,1,0:T(2,128)(2,1)}), bf16[8,2,12288]{2,1,0:T(2,128)(2,1)}, u32[]{:S(2)}, u32[]{:S(2)}) async-start(bf16[8,2,12288]{2,1,0:T(2,128)(2,1)} %reshape.79), calls=%async_computation.2 | async-start | bytes 786432 | tf_op jit(solution)/shard_map/all_to_all | solution.py:43
  117.3 1.6 copy-start.2
  117.3 1.6 copy-start.6
  119.3 1.7 copy-start.8
  120.7 1.3 copy-start.10
  120.7 1.5 copy-start.4
  123.8 7.8 %collective-permute-start.8 = (f32[180,128]{1,0:T(8,128)S(1)}, f32[180,128]{1,0:T(8,128)S(1)}, u32[]{:S(2)}, u32[]{:S(2)}) collective-permute-start(f32[180,128]{1,0:T(8,128)S(1)} %maximum_bitcast_fusion), channel_id=1, source_target_pairs={{0,8},{8,0},{16,24},{24,16},{32,40},{40,32},{48,56},{56,48},{64,72... | collective-permute-start | bytes 276488 | tf_op jit(solution)/shard_map/ppermute | solution.py:30
  123.9 8.4 %collective-permute-start.4 = (bf16[48,8,128]{2,0,1:T(8,128)(2,1)S(1)}, bf16[48,8,128]{2,0,1:T(8,128)(2,1)S(1)}, u32[]{:S(2)}, u32[]{:S(2)}) collective-permute-start(bf16[48,8,128]{2,0,1:T(8,128)(2,1)S(1)} %get-tuple-element.24), channel_id=1, source_target_pairs={{0,8},{8,16},{16,24},{24,32},{32,40},{40,48},{48,56},{56,64},{64,7... | collective-permute-start | bytes 294920 | tf_op jit(solution)/shard_map/ppermute | solution.py:16
  126.3 7.5 %collective-permute-start.5 = (bf16[48,8,128]{2,0,1:T(8,128)(2,1)S(1)}, bf16[48,8,128]{2,0,1:T(8,128)(2,1)S(1)}, u32[]{:S(2)}, u32[]{:S(2)}) collective-permute-start(bf16[48,8,128]{2,0,1:T(8,128)(2,1)S(1)} %get-tuple-element.25), channel_id=1, source_target_pairs={{8,0},{16,8},{24,16},{32,24},{40,32},{48,40},{56,48},{64,56},{72,6... | collective-permute-start | bytes 294920 | tf_op jit(solution)/shard_map/ppermute | solution.py:17
  132.3 22.5 %collective-permute-start.9 = (f32[180,128]{1,0:T(8,128)}, f32[180,128]{1,0:T(8,128)}, u32[]{:S(2)}, u32[]{:S(2)}) collective-permute-start(f32[180,128]{1,0:T(8,128)} %fusion.131), channel_id=1, source_target_pairs={{0,16},{8,24},{16,0},{24,8},{32,48},{40,56},{48,32},{56,40},{64,80... | collective-permute-start | bytes 276488 | tf_op jit(solution)/shard_map/ppermute | solution.py:30
  134.1 9.0 %copy-start.12 = (bf16[3,3,48,48]{3,2,1,0:T(8,128)(2,1)S(1)}, bf16[3,3,48,48]{3,2,1,0:T(8,128)(2,1)}, u32[]{:S(2)}) copy-start(bf16[3,3,48,48]{3,2,1,0:T(8,128)(2,1)} %param.5) | copy-start | bytes 124420
  135.8 14.8 %collective-permute-start.7 = (bf16[48,48,8]{1,2,0:T(8,128)(2,1)S(1)}, bf16[48,48,8]{1,2,0:T(8,128)(2,1)S(1)}, u32[]{:S(2)}, u32[]{:S(2)}) collective-permute-start(bf16[48,48,8]{1,2,0:T(8,128)(2,1)S(1)} %copy.100), channel_id=1, source_target_pairs={{0,1},{1,2},{2,3},{3,4},{4,5},{5,6},{6,7},{8,9},{9,10},{10,11},{11... | collective-permute-start | bytes 110600 | tf_op jit(solution)/shard_map/ppermute | solution.py:16
  139.2 9.2 %collective-permute-start.6 = (bf16[48,48,8]{1,2,0:T(8,128)(2,1)}, bf16[48,48,8]{1,2,0:T(8,128)(2,1)}, u32[]{:S(2)}, u32[]{:S(2)}) collective-permute-start(bf16[48,48,8]{1,2,0:T(8,128)(2,1)} %copy.96), channel_id=1, source_target_pairs={{1,0},{2,1},{3,2},{4,3},{5,4},{6,5},{7,6},{9,8},{10,9},{11,10},{12... | collective-permute-start | bytes 110600 | tf_op jit(solution)/shard_map/ppermute | solution.py:17
  155.7 6.5 %collective-permute-start.10 = (f32[180,128]{1,0:T(8,128)S(1)}, f32[180,128]{1,0:T(8,128)S(1)}, u32[]{:S(2)}, u32[]{:S(2)}) collective-permute-start(f32[180,128]{1,0:T(8,128)S(1)} %fusion.132), channel_id=1, source_target_pairs={{0,32},{8,40},{16,48},{24,56},{32,0},{40,8},{48,16},{56,24},{64,96... | collective-permute-start | bytes 276488 | tf_op jit(solution)/shard_map/ppermute | solution.py:30
  162.2 8.9 %collective-permute-start.11 = (f32[180,128]{1,0:T(8,128)S(1)}, f32[180,128]{1,0:T(8,128)S(1)}, u32[]{:S(2)}, u32[]{:S(2)}) collective-permute-start(f32[180,128]{1,0:T(8,128)S(1)} %add.120), channel_id=1, source_target_pairs={{0,64},{8,72},{16,80},{24,88},{32,96},{40,104},{48,112},{56,120},{... | collective-permute-start | bytes 276488 | tf_op jit(solution)/shard_map/ppermute | solution.py:30
  171.1 4.7 %collective-permute-start.12 = (f32[180,128]{1,0:T(8,128)S(1)}, f32[180,128]{1,0:T(8,128)S(1)}, u32[]{:S(2)}, u32[]{:S(2)}) collective-permute-start(f32[180,128]{1,0:T(8,128)S(1)} %add.121), channel_id=1, source_target_pairs={{0,128},{8,136},{16,144},{24,152},{32,160},{40,168},{48,176},{56,1... | collective-permute-start | bytes 276488 | tf_op jit(solution)/shard_map/ppermute | solution.py:30
  175.8 6.2 %collective-permute-start.13 = (f32[180,128]{1,0:T(8,128)S(1)}, f32[180,128]{1,0:T(8,128)S(1)}, u32[]{:S(2)}, u32[]{:S(2)}) collective-permute-start(f32[180,128]{1,0:T(8,128)S(1)} %add.122), channel_id=1, source_target_pairs={{0,1},{1,0},{2,3},{3,2},{4,5},{5,4},{6,7},{7,6},{8,9},{9,8},{10,11... | collective-permute-start | bytes 276488 | tf_op jit(solution)/shard_map/ppermute | solution.py:30
  182.0 5.6 %collective-permute-start.14 = (f32[180,128]{1,0:T(8,128)S(1)}, f32[180,128]{1,0:T(8,128)S(1)}, u32[]{:S(2)}, u32[]{:S(2)}) collective-permute-start(f32[180,128]{1,0:T(8,128)S(1)} %add.123), channel_id=1, source_target_pairs={{0,2},{1,3},{2,0},{3,1},{4,6},{5,7},{6,4},{7,5},{8,10},{9,11},{10,... | collective-permute-start | bytes 276488 | tf_op jit(solution)/shard_map/ppermute | solution.py:30
  187.5 6.2 %collective-permute-start.15 = (f32[180,128]{1,0:T(8,128)S(1)}, f32[180,128]{1,0:T(8,128)S(1)}, u32[]{:S(2)}, u32[]{:S(2)}) collective-permute-start(f32[180,128]{1,0:T(8,128)S(1)} %add.124), channel_id=1, source_target_pairs={{0,4},{1,5},{2,6},{3,7},{4,0},{5,1},{6,2},{7,3},{8,12},{9,13},{10,... | collective-permute-start | bytes 276488 | tf_op jit(solution)/shard_map/ppermute | solution.py:30

commit v3 on v2

--- a/solution.py
+++ b/solution.py
@@ -19,16 +19,44 @@
     return array
 
 
+RING_DIGITS = {"row": (2, 8, 2), "col": (4, 2)}
+
+
+def gray(value):
+    return value ^ (value >> 1)
+
+
+def gray_inverse(value):
+    result = 0
+    while value:
+        result ^= value
+        value >>= 1
+    return result
+
+
+def ring_partner(index, digits, digit, bit):
+    place = 1
+    for size in digits[digit + 1 :]:
+        place *= size
+    value = index // place % digits[digit]
+    flipped = gray(gray_inverse(value) ^ (1 << bit))
+    return index + (flipped - value) * place
+
+
 def all_sum(x, axes):
     for axis in axes:
         peers = lax.axis_size(axis)
-        if peers & (peers - 1):
+        digits = RING_DIGITS.get(axis, (peers,))
+        product = 1
+        for size in digits:
+            product *= size
+        if product != peers or any(size & (size - 1) for size in digits):
             x = lax.psum(x, axis)
             continue
-        step = 1
-        while step < peers:
-            x = x + lax.ppermute(x, axis, [(i, i ^ step) for i in range(peers)])
-            step *= 2
+        for digit in reversed(range(len(digits))):
+            for bit in range(digits[digit].bit_length() - 1):
+                pairs = [(i, ring_partner(i, digits, digit, bit)) for i in range(peers)]
+                x = x + lax.ppermute(x, axis, pairs)
     return x
 
 

time: 197 us -> 194 us (0.985)
  starting transfers between devices: 83.5 us -> 78.2 us
  waiting for transfers between devices: 55.9 us -> 58.5 us
    ppermute x8, starting transfers between devices: 9.95 us -> 4.65 us  [all_sum(): x = x + lax.ppermute(x, axis, pairs)]
    ppermute x8, waiting for transfers between devices: 18.6 us -> 21.1 us  [all_sum(): x = x + lax.ppermute(x, axis, pairs)]
  transfers between devices with their start and end apart: 22 -> 22, of which waited for: 13 -> 13; matrix products, arithmetic and copies ran while one was open for 25% -> 26% of each run, Pallas kernels for 0% -> 0%
where the time goes in v3:
time: 194 us; the launch traced here: 192 us
  starting transfers between devices  78.2 us (40%)
  waiting for transfers between devices  58.5 us (30%)
  local copies, waits for them, and re-layouts  34.8 us (18%)
  matrix products  11.8 us (6%)
  other arithmetic  7.84 us (4%)
    all_to_all x2, waiting for transfers between devices, mirror_tile(): lax.all_to_all(strip, 'row', split_axis=2, concat_axis=1, tiled=True)  22.2 us
    ppermute x8, waiting for transfers between devices, all_sum(): x = x + lax.ppermute(x, axis, pairs)  21.1 us
    unnamed x37, local copies, waits for them, and re-layouts  19.7 us
    ppermute x4, starting transfers between devices, with_halo(): after = lax.ppermute(initial, axis, down)  18.6 us
    all_to_all x2, starting transfers between devices, mirror_tile(): strip = lax.all_to_all(tile, 'col', split_axis=1, concat_axis=2, tiled=True)  15.6 us
    ppermute x4, starting transfers between devices, with_halo(): before = lax.ppermute(last, axis, up)  14 us
    all_to_all x2, starting transfers between devices, mirror_tile(): lax.all_to_all(turned, 'col', split_axis=2, concat_axis=3, tiled=True)  12.7 us
    all_to_all x2, starting transfers between devices, mirror_tile(): lax.all_to_all(strip, 'row', split_axis=2, concat_axis=1, tiled=True)  12.6 us
  transfers between devices with their start and end apart: 22, of which 13 were waited for; matrix products, arithmetic and copies ran while one was open for 26% of the time, Pallas kernels for 0%

profile of v3, /device:TPU:6, one launch (start us, length us, event | category | flops | bytes accessed | tf_op | source)
XLA Modules:
  0.0 192.5 jit_solution(5246513167016875117)
XLA Ops:
  0.7 1.2 copy_maximum_fusion
  1.9 1.9 collective-permute-start
  3.8 7.5 %collective-permute-start.1 = (bf16[48,8,128]{2,0,1:T(8,128)(2,1)S(1)}, bf16[48,8,128]{2,0,1:T(8,128)(2,1)S(1)}, u32[]{:S(2)}, u32[]{:S(2)}) collective-permute-start(bf16[48,8,128]{2,0,1:T(8,128)(2,1)S(1)} %get-tuple-element.27), channel_id=1, source_target_pairs={{8,0},{16,8},{24,16},{32,24},{40,32},{48,40},{56,48},{64,56},{72,6... | collective-permute-start | bytes 294920 | tf_op jit(solution)/shard_map/ppermute | solution.py:17
  11.3 0.9 copy.88
  12.2 7.4 %all-to-all-start.3 = ((bf16[48,32,128]{2,0,1:T(8,128)(2,1)}), bf16[48,32,128]{2,0,1:T(8,128)(2,1)S(1)}, u32[]{:S(2)}, u32[]{:S(2)}) async-start(bf16[48,32,128]{2,0,1:T(8,128)(2,1)} %copy.88), calls=%async_computation.3 | async-start | bytes 786432 | tf_op jit(solution)/shard_map/all_to_all | solution.py:68
  20.0 0.5 copy.68
  21.0 1.9 collective-permute-start.3
  22.9 6.3 %collective-permute-start.2 = (bf16[48,48,8]{1,2,0:T(8,128)(2,1)S(1)}, bf16[48,48,8]{1,2,0:T(8,128)(2,1)S(1)}, u32[]{:S(2)}, u32[]{:S(2)}) collective-permute-start(bf16[48,48,8]{1,2,0:T(8,128)(2,1)S(1)} %copy.68), channel_id=1, source_target_pairs={{0,1},{1,2},{2,3},{3,4},{4,5},{5,6},{6,7},{8,9},{9,10},{10,11},{11... | collective-permute-start | bytes 110600 | tf_op jit(solution)/shard_map/ppermute | solution.py:16
  29.5 1.9 collective-permute-done.2
  32.4 0.8 maximum_maximum_fusion
  34.6 0.7 copy-done.3
  36.5 0.7 copy-done.5
  37.3 1.0 fusion.12
  38.3 8.2 %all-to-all-start = ((bf16[48,32,128]{2,0,1:T(8,128)(2,1)}), bf16[48,32,128]{2,0,1:T(8,128)(2,1)S(1)}, u32[]{:S(2)}, u32[]{:S(2)}) async-start(bf16[48,32,128]{2,0,1:T(8,128)(2,1)} %fusion.12), calls=%async_computation | async-start | bytes 786432 | tf_op jit(solution)/shard_map/all_to_all | solution.py:68
  46.5 0.7 copy.91
  47.2 2.5 %reshape.81 = bf16[32,2,3072]{2,1,0:T(2,128)(2,1)} reshape(bf16[1024,4,48]{2,1,0:T(4,128)(2,1)S(1)} %bitcast.228) | data formatting | bytes 786432
  49.6 3.7 %all-to-all-done = bf16[48,32,128]{2,0,1:T(8,128)(2,1)S(1)} async-done(((bf16[48,32,128]{2,0,1:T(8,128)(2,1)}), bf16[48,32,128]{2,0,1:T(8,128)(2,1)S(1)}, u32[]{:S(2)}, u32[]{:S(2)}) %all-to-all-start) | async-done | bytes 393248 | tf_op jit(solution)/shard_map/all_to_all | solution.py:68
  53.3 7.5 %all-to-all-start.4 = ((bf16[32,2,3072]{2,1,0:T(2,128)(2,1)}), bf16[32,2,3072]{2,1,0:T(2,128)(2,1)S(1)}, u32[]{:S(2)}, u32[]{:S(2)}) async-start(bf16[32,2,3072]{2,1,0:T(2,128)(2,1)} %reshape.81), calls=%async_computation.4 | async-start | bytes 786432 | tf_op jit(solution)/shard_map/all_to_all | solution.py:69
  60.8 0.7 copy.122
  61.5 2.5 %reshape.77 = bf16[32,2,3072]{2,1,0:T(2,128)(2,1)} reshape(bf16[1024,4,48]{2,1,0:T(4,128)(2,1)S(1)} %bitcast.229) | data formatting | bytes 786432
  63.9 11.4 %all-to-all-done.4 = bf16[32,2,3072]{2,1,0:T(2,128)(2,1)S(1)} async-done(((bf16[32,2,3072]{2,1,0:T(2,128)(2,1)}), bf16[32,2,3072]{2,1,0:T(2,128)(2,1)S(1)}, u32[]{:S(2)}, u32[]{:S(2)}) %all-to-all-start.4) | async-done | bytes 393248 | tf_op jit(solution)/shard_map/all_to_all | solution.py:69
  75.3 5.2 %all-to-all-start.1 = ((bf16[32,2,3072]{2,1,0:T(2,128)(2,1)}), bf16[32,2,3072]{2,1,0:T(2,128)(2,1)S(1)}, u32[]{:S(2)}, u32[]{:S(2)}) async-start(bf16[32,2,3072]{2,1,0:T(2,128)(2,1)} %reshape.77), calls=%async_computation.1 | async-start | bytes 786432 | tf_op jit(solution)/shard_map/all_to_all | solution.py:69
  80.5 1.1 reshape.82
  81.8 2.3 %reshape.83 = bf16[8,2,12288]{2,1,0:T(2,128)(2,1)} reshape(bf16[32,4,32,48]{3,2,1,0:T(8,128)(2,1)S(1)} %bitcast.231) | data formatting | bytes 786432
  84.1 10.8 %all-to-all-done.1 = bf16[32,2,3072]{2,1,0:T(2,128)(2,1)S(1)} async-done(((bf16[32,2,3072]{2,1,0:T(2,128)(2,1)}), bf16[32,2,3072]{2,1,0:T(2,128)(2,1)S(1)}, u32[]{:S(2)}, u32[]{:S(2)}) %all-to-all-start.1) | async-done | bytes 393248 | tf_op jit(solution)/shard_map/all_to_all | solution.py:69
  94.9 6.0 %all-to-all-start.5 = ((bf16[8,2,12288]{2,1,0:T(2,128)(2,1)}), bf16[8,2,12288]{2,1,0:T(2,128)(2,1)S(1)}, u32[]{:S(2)}, u32[]{:S(2)}) async-start(bf16[8,2,12288]{2,1,0:T(2,128)(2,1)} %reshape.83), calls=%async_computation.5 | async-start | bytes 786432 | tf_op jit(solution)/shard_map/all_to_all | solution.py:71
  100.9 1.1 reshape.78
  102.2 2.3 %reshape.79 = bf16[8,2,12288]{2,1,0:T(2,128)(2,1)} reshape(bf16[32,4,32,48]{3,2,1,0:T(8,128)(2,1)S(1)} %bitcast.233) | data formatting | bytes 786432
  104.5 3.3 %all-to-all-done.5 = bf16[8,2,12288]{2,1,0:T(2,128)(2,1)S(1)} async-done(((bf16[8,2,12288]{2,1,0:T(2,128)(2,1)}), bf16[8,2,12288]{2,1,0:T(2,128)(2,1)S(1)}, u32[]{:S(2)}, u32[]{:S(2)}) %all-to-all-start.5) | async-done | bytes 393248 | tf_op jit(solution)/shard_map/all_to_all | solution.py:71
  107.8 6.7 %all-to-all-start.2 = ((bf16[8,2,12288]{2,1,0:T(2,128)(2,1)}), bf16[8,2,12288]{2,1,0:T(2,128)(2,1)}, u32[]{:S(2)}, u32[]{:S(2)}) async-start(bf16[8,2,12288]{2,1,0:T(2,128)(2,1)} %reshape.79), calls=%async_computation.2 | async-start | bytes 786432 | tf_op jit(solution)/shard_map/all_to_all | solution.py:71
  114.4 1.1 reshape.84
  116.0 1.3 copy.95
  117.3 1.6 convolution_bitcast_fusion.3
  119.4 1.3 fusion.21
  121.3 0.7 copy-done.10
  123.9 2.4 %collective-permute-start.4 = (bf16[48,8,128]{2,0,1:T(8,128)(2,1)S(1)}, bf16[48,8,128]{2,0,1:T(8,128)(2,1)S(1)}, u32[]{:S(2)}, u32[]{:S(2)}) collective-permute-start(bf16[48,8,128]{2,0,1:T(8,128)(2,1)S(1)} %get-tuple-element.24), channel_id=1, source_target_pairs={{0,8},{8,16},{16,24},{24,32},{32,40},{40,48},{48,56},{56,64},{64,7... | collective-permute-start | bytes 294920 | tf_op jit(solution)/shard_map/ppermute | solution.py:16
  126.3 5.3 %collective-permute-start.5 = (bf16[48,8,128]{2,0,1:T(8,128)(2,1)S(1)}, bf16[48,8,128]{2,0,1:T(8,128)(2,1)S(1)}, u32[]{:S(2)}, u32[]{:S(2)}) collective-permute-start(bf16[48,8,128]{2,0,1:T(8,128)(2,1)S(1)} %get-tuple-element.25), channel_id=1, source_target_pairs={{8,0},{16,8},{24,16},{32,24},{40,32},{48,40},{56,48},{64,56},{72,6... | collective-permute-start | bytes 294920 | tf_op jit(solution)/shard_map/ppermute | solution.py:17
  131.6 0.7 fusion.131
  132.3 1.5 collective-permute-done.5
  134.1 1.2 copy.96
  135.8 3.4 %collective-permute-start.7 = (bf16[48,48,8]{1,2,0:T(8,128)(2,1)S(1)}, bf16[48,48,8]{1,2,0:T(8,128)(2,1)S(1)}, u32[]{:S(2)}, u32[]{:S(2)}) collective-permute-start(bf16[48,48,8]{1,2,0:T(8,128)(2,1)S(1)} %copy.100), channel_id=1, source_target_pairs={{0,1},{1,2},{2,3},{3,4},{4,5},{5,6},{6,7},{8,9},{9,10},{10,11},{11... | collective-permute-start | bytes 110600 | tf_op jit(solution)/shard_map/ppermute | solution.py:16
  139.2 4.0 %collective-permute-start.6 = (bf16[48,48,8]{1,2,0:T(8,128)(2,1)}, bf16[48,48,8]{1,2,0:T(8,128)(2,1)}, u32[]{:S(2)}, u32[]{:S(2)}) collective-permute-start(bf16[48,48,8]{1,2,0:T(8,128)(2,1)} %copy.96), channel_id=1, source_target_pairs={{1,0},{2,1},{3,2},{4,3},{5,4},{6,5},{7,6},{9,8},{10,9},{11,10},{12... | collective-permute-start | bytes 110600 | tf_op jit(solution)/shard_map/ppermute | solution.py:17
  143.6 4.8 %collective-permute-done.6 = bf16[48,48,8]{1,2,0:T(8,128)(2,1)} collective-permute-done((bf16[48,48,8]{1,2,0:T(8,128)(2,1)}, bf16[48,48,8]{1,2,0:T(8,128)(2,1)}, u32[]{:S(2)}, u32[]{:S(2)}) %collective-permute-start.6) | collective-permute-done | bytes 36896 | tf_op jit(solution)/shard_map/ppermute | solution.py:17
  148.4 2.2 %copy.97 = bf16[48,48,8]{2,0,1:T(8,128)(2,1)} copy(bf16[48,48,8]{1,2,0:T(8,128)(2,1)} %collective-permute-done.6) | data formatting | bytes 73728 | tf_op jit(solution)/shard_map/ppermute | solution.py:17
  150.5 1.3 copy.101
  151.8 2.0 %pad_maximum_fusion.1 = (bf16[48,48,136]{2,0,1:T(8,128)(2,1)S(1)}, bf16[48,48,136]{2,0,1:T(8,128)(2,1)S(1)}) fusion(bf16[48,48,8]{2,0,1:T(8,128)(2,1)} %copy.97, bf16[48,8,128]{2,0,1:T(8,128)(2,1)S(1)} %collective-permute-done.5, bf16[48,32,128]{2,0,1:T(8,128)(2,1)S(1)} %fusion.8, bf16[48,8,128]{2,0,1:T(8,128)(2,1)S(1)} %collective-permute-done.4, ...), kind=kLoop, calls=%fused_computation.32 | loop fusion | flops 5013504 | bytes 1916928 | tf_op jit(solution)/shard_map/concatenate | solution.py:18
  154.8 0.9 fusion.132
  155.7 0.6 collective-permute-start.10
  156.5 5.7 %collective-permute-done.10 = f32[180,128]{1,0:T(8,128)S(1)} collective-permute-done((f32[180,128]{1,0:T(8,128)S(1)}, f32[180,128]{1,0:T(8,128)S(1)}, u32[]{:S(2)}, u32[]{:S(2)}) %collective-permute-start.10) | collective-permute-done | bytes 92192 | tf_op jit(solution)/shard_map/ppermute | solution.py:59
  162.9 6.0 %collective-permute-done.11 = f32[180,128]{1,0:T(8,128)S(1)} collective-permute-done((f32[180,128]{1,0:T(8,128)S(1)}, f32[180,128]{1,0:T(8,128)S(1)}, u32[]{:S(2)}, u32[]{:S(2)}) %collective-permute-start.11) | collective-permute-done | bytes 92192 | tf_op jit(solution)/shard_map/ppermute | solution.py:59
  169.3 4.9 %collective-permute-done.12 = f32[180,128]{1,0:T(8,128)S(1)} collective-permute-done((f32[180,128]{1,0:T(8,128)S(1)}, f32[180,128]{1,0:T(8,128)S(1)}, u32[]{:S(2)}, u32[]{:S(2)}) %collective-permute-start.12) | collective-permute-done | bytes 92192 | tf_op jit(solution)/shard_map/ppermute | solution.py:59
  174.2 0.6 collective-permute-start.13
  174.8 0.6 fusion.9
  175.4 2.3 %reshape.80 = bf16[32,4,32,48]{3,2,1,0:T(8,128)(2,1)S(1)} reshape(bf16[8,2,12288]{2,1,0:T(2,128)(2,1)} %all-to-all-done.2) | data formatting | bytes 786432
  177.7 2.7 %collective-permute-done.13 = f32[180,128]{1,0:T(8,128)S(1)} collective-permute-done((f32[180,128]{1,0:T(8,128)S(1)}, f32[180,128]{1,0:T(8,128)S(1)}, u32[]{:S(2)}, u32[]{:S(2)}) %collective-permute-start.13) | collective-permute-done | bytes 92192 | tf_op jit(solution)/shard_map/ppermute | solution.py:59
  180.4 1.6 collective-permute-start.14
  182.5 2.2 %copy.87 = f32[48,32,128]{2,0,1:T(8,128)} copy(f32[48,32,128]{0,1,2:T(8,128)S(1)} %bitcast.225) | data formatting | bytes 1572864 | tf_op jit(solution)/shard_map/convert_element_type | solution.py:99
  185.1 1.2 collective-permute-start.15
  186.3 1.5 add_convert_fusion
  187.7 0.8 copy.110
  188.6 0.8 copy.109
  189.4 1.5 collective-permute-done.15
  191.0 0.7 div.21
  191.7 0.8 div.18
  (90 shorter events, 12.9 us)
Async XLA Ops:
  0.6 36.6 %copy-start = (bf16[48,48]{1,0:T(8,128)(2,1)S(1)}, bf16[48,48]{1,0:T(8,128)(2,1)}, u32[]{:S(2)}) copy-start(bf16[48,48]{1,0:T(8,128)(2,1)} %param.6) | copy-start | bytes 13828
  0.6 10.6 %copy-start.1 = (bf16[48,32,128]{2,1,0:T(8,128)(2,1)S(1)}, bf16[48,32,128]{2,1,0:T(8,128)(2,1)}, u32[]{:S(2)}) copy-start(bf16[48,32,128]{2,1,0:T(8,128)(2,1)} %param.7) | copy-start | bytes 1179652
  1.9 17.8 %collective-permute-start = (bf16[48,8,128]{2,0,1:T(8,128)(2,1)S(1)}, bf16[48,8,128]{2,0,1:T(8,128)(2,1)S(1)}, u32[]{:S(2)}, u32[]{:S(2)}) collective-permute-start(bf16[48,8,128]{2,0,1:T(8,128)(2,1)S(1)} %get-tuple-element.26), channel_id=1, source_target_pairs={{0,8},{8,16},{16,24},{24,32},{32,40},{40,48},{48,56},{56,64},{64,7... | collective-permute-start | bytes 294920 | tf_op jit(solution)/shard_map/ppermute | solution.py:16
  3.8 15.8 %collective-permute-start.1 = (bf16[48,8,128]{2,0,1:T(8,128)(2,1)S(1)}, bf16[48,8,128]{2,0,1:T(8,128)(2,1)S(1)}, u32[]{:S(2)}, u32[]{:S(2)}) collective-permute-start(bf16[48,8,128]{2,0,1:T(8,128)(2,1)S(1)} %get-tuple-element.27), channel_id=1, source_target_pairs={{8,0},{16,8},{24,16},{32,24},{40,32},{48,40},{56,48},{64,56},{72,6... | collective-permute-start | bytes 294920 | tf_op jit(solution)/shard_map/ppermute | solution.py:17
  12.2 26.1 %all-to-all-start.3 = ((bf16[48,32,128]{2,0,1:T(8,128)(2,1)}), bf16[48,32,128]{2,0,1:T(8,128)(2,1)S(1)}, u32[]{:S(2)}, u32[]{:S(2)}) async-start(bf16[48,32,128]{2,0,1:T(8,128)(2,1)} %copy.88), calls=%async_computation.3 | async-start | bytes 786432 | tf_op jit(solution)/shard_map/all_to_all | solution.py:68
  19.9 9.3 %copy-start.11 = (bf16[3,3,48,48]{3,2,1,0:T(8,128)(2,1)S(1)}, bf16[3,3,48,48]{3,2,1,0:T(8,128)(2,1)}, u32[]{:S(2)}) copy-start(bf16[3,3,48,48]{3,2,1,0:T(8,128)(2,1)} %param.5) | copy-start | bytes 124420
  21.0 10.9 %collective-permute-start.3 = (bf16[48,48,8]{1,2,0:T(8,128)(2,1)S(1)}, bf16[48,48,8]{1,2,0:T(8,128)(2,1)S(1)}, u32[]{:S(2)}, u32[]{:S(2)}) collective-permute-start(bf16[48,48,8]{1,2,0:T(8,128)(2,1)S(1)} %copy.72), channel_id=1, source_target_pairs={{1,0},{2,1},{3,2},{4,3},{5,4},{6,5},{7,6},{9,8},{10,9},{11,10},{12... | collective-permute-start | bytes 110600 | tf_op jit(solution)/shard_map/ppermute | solution.py:17
  22.9 8.5 %collective-permute-start.2 = (bf16[48,48,8]{1,2,0:T(8,128)(2,1)S(1)}, bf16[48,48,8]{1,2,0:T(8,128)(2,1)S(1)}, u32[]{:S(2)}, u32[]{:S(2)}) collective-permute-start(bf16[48,48,8]{1,2,0:T(8,128)(2,1)S(1)} %copy.68), channel_id=1, source_target_pairs={{0,1},{1,2},{2,3},{3,4},{4,5},{5,6},{6,7},{8,9},{9,10},{10,11},{11... | collective-permute-start | bytes 110600 | tf_op jit(solution)/shard_map/ppermute | solution.py:16
  33.3 2.3 %copy-start.7 = (bf16[48,48,136]{2,0,1:T(8,128)(2,1)}, bf16[48,48,136]{2,0,1:T(8,128)(2,1)S(1)}, u32[]{:S(2)}) copy-start(bf16[48,48,136]{2,0,1:T(8,128)(2,1)S(1)} %get-tuple-element.21) | copy-start | bytes 1880068
  33.3 2.6 %copy-start.9 = (bf16[48,48,136]{2,0,1:T(8,128)(2,1)}, bf16[48,48,136]{2,0,1:T(8,128)(2,1)S(1)}, u32[]{:S(2)}) copy-start(bf16[48,48,136]{2,0,1:T(8,128)(2,1)S(1)} %get-tuple-element.20) | copy-start | bytes 1880068
  34.3 1.0 copy-start.3
  36.5 0.8 copy-start.5
  38.3 15.0 %all-to-all-start = ((bf16[48,32,128]{2,0,1:T(8,128)(2,1)}), bf16[48,32,128]{2,0,1:T(8,128)(2,1)S(1)}, u32[]{:S(2)}, u32[]{:S(2)}) async-start(bf16[48,32,128]{2,0,1:T(8,128)(2,1)} %fusion.12), calls=%async_computation | async-start | bytes 786432 | tf_op jit(solution)/shard_map/all_to_all | solution.py:68
  53.3 22.0 %all-to-all-start.4 = ((bf16[32,2,3072]{2,1,0:T(2,128)(2,1)}), bf16[32,2,3072]{2,1,0:T(2,128)(2,1)S(1)}, u32[]{:S(2)}, u32[]{:S(2)}) async-start(bf16[32,2,3072]{2,1,0:T(2,128)(2,1)} %reshape.81), calls=%async_computation.4 | async-start | bytes 786432 | tf_op jit(solution)/shard_map/all_to_all | solution.py:69
  75.3 19.6 %all-to-all-start.1 = ((bf16[32,2,3072]{2,1,0:T(2,128)(2,1)}), bf16[32,2,3072]{2,1,0:T(2,128)(2,1)S(1)}, u32[]{:S(2)}, u32[]{:S(2)}) async-start(bf16[32,2,3072]{2,1,0:T(2,128)(2,1)} %reshape.77), calls=%async_computation.1 | async-start | bytes 786432 | tf_op jit(solution)/shard_map/all_to_all | solution.py:69
  94.9 12.9 %all-to-all-start.5 = ((bf16[8,2,12288]{2,1,0:T(2,128)(2,1)}), bf16[8,2,12288]{2,1,0:T(2,128)(2,1)S(1)}, u32[]{:S(2)}, u32[]{:S(2)}) async-start(bf16[8,2,12288]{2,1,0:T(2,128)(2,1)} %reshape.83), calls=%async_computation.5 | async-start | bytes 786432 | tf_op jit(solution)/shard_map/all_to_all | solution.py:71
  107.8 67.6 %all-to-all-start.2 = ((bf16[8,2,12288]{2,1,0:T(2,128)(2,1)}), bf16[8,2,12288]{2,1,0:T(2,128)(2,1)}, u32[]{:S(2)}, u32[]{:S(2)}) async-start(bf16[8,2,12288]{2,1,0:T(2,128)(2,1)} %reshape.79), calls=%async_computation.2 | async-start | bytes 786432 | tf_op jit(solution)/shard_map/all_to_all | solution.py:71
  117.3 1.6 copy-start.2
  117.3 1.6 copy-start.6
  119.3 1.7 copy-start.8
  120.7 1.3 copy-start.10
  120.7 1.5 copy-start.4
  123.8 7.8 %collective-permute-start.8 = (f32[180,128]{1,0:T(8,128)S(1)}, f32[180,128]{1,0:T(8,128)S(1)}, u32[]{:S(2)}, u32[]{:S(2)}) collective-permute-start(f32[180,128]{1,0:T(8,128)S(1)} %maximum_bitcast_fusion), channel_id=1, source_target_pairs={{0,8},{8,0},{16,24},{24,16},{32,40},{40,32},{48,56},{56,48},{64,72... | collective-permute-start | bytes 276488 | tf_op jit(solution)/shard_map/ppermute | solution.py:59
  123.9 8.4 %collective-permute-start.4 = (bf16[48,8,128]{2,0,1:T(8,128)(2,1)S(1)}, bf16[48,8,128]{2,0,1:T(8,128)(2,1)S(1)}, u32[]{:S(2)}, u32[]{:S(2)}) collective-permute-start(bf16[48,8,128]{2,0,1:T(8,128)(2,1)S(1)} %get-tuple-element.24), channel_id=1, source_target_pairs={{0,8},{8,16},{16,24},{24,32},{32,40},{40,48},{48,56},{56,64},{64,7... | collective-permute-start | bytes 294920 | tf_op jit(solution)/shard_map/ppermute | solution.py:16
  126.3 7.5 %collective-permute-start.5 = (bf16[48,8,128]{2,0,1:T(8,128)(2,1)S(1)}, bf16[48,8,128]{2,0,1:T(8,128)(2,1)S(1)}, u32[]{:S(2)}, u32[]{:S(2)}) collective-permute-start(bf16[48,8,128]{2,0,1:T(8,128)(2,1)S(1)} %get-tuple-element.25), channel_id=1, source_target_pairs={{8,0},{16,8},{24,16},{32,24},{40,32},{48,40},{56,48},{64,56},{72,6... | collective-permute-start | bytes 294920 | tf_op jit(solution)/shard_map/ppermute | solution.py:17
  132.3 22.5 %collective-permute-start.9 = (f32[180,128]{1,0:T(8,128)}, f32[180,128]{1,0:T(8,128)}, u32[]{:S(2)}, u32[]{:S(2)}) collective-permute-start(f32[180,128]{1,0:T(8,128)} %fusion.131), channel_id=1, source_target_pairs={{0,16},{8,24},{16,0},{24,8},{32,48},{40,56},{48,32},{56,40},{64,80... | collective-permute-start | bytes 276488 | tf_op jit(solution)/shard_map/ppermute | solution.py:59
  134.1 9.0 %copy-start.12 = (bf16[3,3,48,48]{3,2,1,0:T(8,128)(2,1)S(1)}, bf16[3,3,48,48]{3,2,1,0:T(8,128)(2,1)}, u32[]{:S(2)}) copy-start(bf16[3,3,48,48]{3,2,1,0:T(8,128)(2,1)} %param.5) | copy-start | bytes 124420
  135.8 14.8 %collective-permute-start.7 = (bf16[48,48,8]{1,2,0:T(8,128)(2,1)S(1)}, bf16[48,48,8]{1,2,0:T(8,128)(2,1)S(1)}, u32[]{:S(2)}, u32[]{:S(2)}) collective-permute-start(bf16[48,48,8]{1,2,0:T(8,128)(2,1)S(1)} %copy.100), channel_id=1, source_target_pairs={{0,1},{1,2},{2,3},{3,4},{4,5},{5,6},{6,7},{8,9},{9,10},{10,11},{11... | collective-permute-start | bytes 110600 | tf_op jit(solution)/shard_map/ppermute | solution.py:16
  139.2 9.2 %collective-permute-start.6 = (bf16[48,48,8]{1,2,0:T(8,128)(2,1)}, bf16[48,48,8]{1,2,0:T(8,128)(2,1)}, u32[]{:S(2)}, u32[]{:S(2)}) collective-permute-start(bf16[48,48,8]{1,2,0:T(8,128)(2,1)} %copy.96), channel_id=1, source_target_pairs={{1,0},{2,1},{3,2},{4,3},{5,4},{6,5},{7,6},{9,8},{10,9},{11,10},{12... | collective-permute-start | bytes 110600 | tf_op jit(solution)/shard_map/ppermute | solution.py:17
  155.7 6.5 %collective-permute-start.10 = (f32[180,128]{1,0:T(8,128)S(1)}, f32[180,128]{1,0:T(8,128)S(1)}, u32[]{:S(2)}, u32[]{:S(2)}) collective-permute-start(f32[180,128]{1,0:T(8,128)S(1)} %fusion.132), channel_id=1, source_target_pairs={{0,48},{8,56},{16,32},{24,40},{32,16},{40,24},{48,0},{56,8},{64,11... | collective-permute-start | bytes 276488 | tf_op jit(solution)/shard_map/ppermute | solution.py:59
  162.1 6.8 %collective-permute-start.11 = (f32[180,128]{1,0:T(8,128)S(1)}, f32[180,128]{1,0:T(8,128)S(1)}, u32[]{:S(2)}, u32[]{:S(2)}) collective-permute-start(f32[180,128]{1,0:T(8,128)S(1)} %add.120), channel_id=1, source_target_pairs={{0,96},{8,104},{16,112},{24,120},{32,64},{40,72},{48,80},{56,88},{... | collective-permute-start | bytes 276488 | tf_op jit(solution)/shard_map/ppermute | solution.py:59
  168.9 5.3 %collective-permute-start.12 = (f32[180,128]{1,0:T(8,128)S(1)}, f32[180,128]{1,0:T(8,128)S(1)}, u32[]{:S(2)}, u32[]{:S(2)}) collective-permute-start(f32[180,128]{1,0:T(8,128)S(1)} %add.121), channel_id=1, source_target_pairs={{0,128},{8,136},{16,144},{24,152},{32,160},{40,168},{48,176},{56,1... | collective-permute-start | bytes 276488 | tf_op jit(solution)/shard_map/ppermute | solution.py:59
  174.2 6.2 %collective-permute-start.13 = (f32[180,128]{1,0:T(8,128)S(1)}, f32[180,128]{1,0:T(8,128)S(1)}, u32[]{:S(2)}, u32[]{:S(2)}) collective-permute-start(f32[180,128]{1,0:T(8,128)S(1)} %add.122), channel_id=1, source_target_pairs={{0,1},{1,0},{2,3},{3,2},{4,5},{5,4},{6,7},{7,6},{8,9},{9,8},{10,11... | collective-permute-start | bytes 276488 | tf_op jit(solution)/shard_map/ppermute | solution.py:59
  180.4 4.7 %collective-permute-start.14 = (f32[180,128]{1,0:T(8,128)S(1)}, f32[180,128]{1,0:T(8,128)S(1)}, u32[]{:S(2)}, u32[]{:S(2)}) collective-permute-start(f32[180,128]{1,0:T(8,128)S(1)} %add.123), channel_id=1, source_target_pairs={{0,2},{1,3},{2,0},{3,1},{4,6},{5,7},{6,4},{7,5},{8,10},{9,11},{10,... | collective-permute-start | bytes 276488 | tf_op jit(solution)/shard_map/ppermute | solution.py:59
  185.1 5.9 %collective-permute-start.15 = (f32[180,128]{1,0:T(8,128)S(1)}, f32[180,128]{1,0:T(8,128)S(1)}, u32[]{:S(2)}, u32[]{:S(2)}) collective-permute-start(f32[180,128]{1,0:T(8,128)S(1)} %add.124), channel_id=1, source_target_pairs={{0,6},{1,7},{2,4},{3,5},{4,2},{5,3},{6,0},{7,1},{8,14},{9,15},{10,... | collective-permute-start | bytes 276488 | tf_op jit(solution)/shard_map/ppermute | solution.py:59

commit v4 on v3

--- a/solution.py
+++ b/solution.py
@@ -81,13 +81,11 @@
     map_bins = rows * lax.axis_size("row")
     active = jnp.maximum(maps, 0)
     padded = with_halo(active, (("row", 1), ("col", 2)), DILATION)
-    before = jnp.zeros((chans, rows, cols), jnp.float32)
-    for row_tap in range(3):
-        for col_tap in range(3):
-            piece = window(padded, DILATION * row_tap, DILATION * col_tap, rows, cols)
-            before = before + jnp.einsum(
-                "io,ihw->ohw", kernel[row_tap, col_tap], piece, preferred_element_type=jnp.float32
-            )
+    taps = kernel.reshape(9, chans, chans)
+    pieces = jnp.stack(
+        [window(padded, DILATION * a, DILATION * b, rows, cols) for a in range(3) for b in range(3)]
+    )
+    before = jnp.einsum("tio,tihw->ohw", taps, pieces, preferred_element_type=jnp.float32)
     hidden = jnp.maximum(before, 0.0).astype(jnp.bfloat16)
     mixed = jnp.einsum("io,ihw->ohw", mixing, hidden, preferred_element_type=jnp.float32).astype(
         jnp.bfloat16
@@ -103,32 +101,20 @@
     local_mixing = jnp.einsum("ihw,ohw->io", hidden, grad_mixed, preferred_element_type=jnp.float32)
     grad_hidden = jnp.einsum("io,ohw->ihw", mixing, grad_mixed, preferred_element_type=jnp.float32)
     grad_before = jnp.where(hidden > 0, grad_hidden, 0.0).astype(jnp.bfloat16)
-    tap_grads = []
-    for row_tap in range(3):
-        for col_tap in range(3):
-            piece = window(padded, DILATION * row_tap, DILATION * col_tap, rows, cols)
-            tap_grads.append(
-                jnp.einsum("ihw,ohw->io", piece, grad_before, preferred_element_type=jnp.float32)
-            )
-    local_kernel = jnp.stack(tap_grads).reshape(3, 3, chans, chans)
+    local_kernel = jnp.einsum("tihw,ohw->tio", pieces, grad_before, preferred_element_type=jnp.float32)
     flat = jnp.concatenate([local_kernel.reshape(-1), local_mixing.reshape(-1)])
     sums = all_sum(flat.reshape(-1, 128), ("row", "col")).reshape(-1)
     grad_kernel = sums[: 9 * chans * chans].reshape(3, 3, chans, chans)
     grad_mixing = sums[9 * chans * chans :].reshape(chans, chans)
     grad_padded = with_halo(grad_before, (("row", 1), ("col", 2)), DILATION)
-    grad_active = jnp.zeros((chans, rows, cols), jnp.float32)
-    for row_tap in range(3):
-        for col_tap in range(3):
-            piece = window(
-                grad_padded,
-                2 * DILATION - DILATION * row_tap,
-                2 * DILATION - DILATION * col_tap,
-                rows,
-                cols,
-            )
-            grad_active = grad_active + jnp.einsum(
-                "io,ohw->ihw", kernel[row_tap, col_tap], piece, preferred_element_type=jnp.float32
-            )
+    grad_pieces = jnp.stack(
+        [
+            window(grad_padded, 2 * DILATION - DILATION * a, 2 * DILATION - DILATION * b, rows, cols)
+            for a in range(3)
+            for b in range(3)
+        ]
+    )
+    grad_active = jnp.einsum("tio,tohw->ihw", taps, grad_pieces, preferred_element_type=jnp.float32)
     grad_maps = (grad_wide + jnp.where(maps > 0, grad_active, 0.0)).astype(jnp.bfloat16)
     return (output, grad_maps, grad_kernel / map_bins, grad_mixing / map_bins)
 

time: 194 us -> 185 us (0.954)
  matrix products: 11.8 us -> 7.42 us
  waiting for transfers between devices: 58.5 us -> 55.6 us
  local copies, waits for them, and re-layouts: 34.8 us -> 32.8 us
    dot_general x27 -> x3, matrix products: 8.85 us -> 3.48 us  [the longest x1 1.67 us: shards(): jnp.einsum('tio,tohw->ihw', taps, grad_pieces, preferred_element_type=jnp...]
    ppermute x8, starting transfers between devices: 4.65 us -> 7.09 us  [all_sum(): x = x + lax.ppermute(x, axis, pairs)]
    ppermute x4, waiting for transfers between devices: 6.27 us -> 3.86 us  [with_halo(): after = lax.ppermute(initial, axis, down)]
    unnamed x37 -> x40, local copies, waits for them, and re-layouts: 19.7 us -> 21.4 us
  transfers between devices with their start and end apart: 22 -> 22, of which waited for: 13 -> 15; matrix products, arithmetic and copies ran while one was open for 26% -> 22% of each run, Pallas kernels for 0% -> 0%
where the time goes in v4:
time: 185 us; the launch traced here: 183 us
  starting transfers between devices  79.8 us (43%)
  waiting for transfers between devices  55.6 us (30%)
  local copies, waits for them, and re-layouts  32.8 us (18%)
  matrix products  7.42 us (4%)
  other arithmetic  6.13 us (3%)
    all_to_all x2, waiting for transfers between devices, mirror_tile(): lax.all_to_all(strip, 'row', split_axis=2, concat_axis=1, tiled=True)  22.2 us
    unnamed x40, local copies, waits for them, and re-layouts  21.4 us
    ppermute x8, waiting for transfers between devices, all_sum(): x = x + lax.ppermute(x, axis, pairs)  20.9 us
    ppermute x4, starting transfers between devices, with_halo(): after = lax.ppermute(initial, axis, down)  18.7 us
    all_to_all x2, starting transfers between devices, mirror_tile(): strip = lax.all_to_all(tile, 'col', split_axis=1, concat_axis=2, tiled=True)  14.6 us
    ppermute x4, starting transfers between devices, with_halo(): before = lax.ppermute(last, axis, up)  14.1 us
    all_to_all x2, starting transfers between devices, mirror_tile(): lax.all_to_all(turned, 'col', split_axis=2, concat_axis=3, tiled=True)  12.7 us
    all_to_all x2, starting transfers between devices, mirror_tile(): lax.all_to_all(strip, 'row', split_axis=2, concat_axis=1, tiled=True)  12.6 us
  transfers between devices with their start and end apart: 22, of which 15 were waited for; matrix products, arithmetic and copies ran while one was open for 22% of the time, Pallas kernels for 0%

profile of v4, /device:TPU:6, one launch (start us, length us, event | category | flops | bytes accessed | tf_op | source)
XLA Modules:
  0.0 183.1 jit_solution(5321396697866781287)
XLA Ops:
  0.6 1.2 copy_maximum_fusion
  1.8 1.9 %collective-permute-start = (bf16[48,8,128]{2,0,1:T(8,128)(2,1)S(1)}, bf16[48,8,128]{2,0,1:T(8,128)(2,1)S(1)}, u32[]{:S(2)}, u32[]{:S(2)}) collective-permute-start(bf16[48,8,128]{2,0,1:T(8,128)(2,1)S(1)} %get-tuple-element.26), channel_id=1, source_target_pairs={{0,8},{8,16},{16,24},{24,32},{32,40},{40,48},{48,56},{56,64},{64,7... | collective-permute-start | bytes 294920 | tf_op jit(solution)/shard_map/ppermute | solution.py:16
  3.8 7.6 %collective-permute-start.1 = (bf16[48,8,128]{2,0,1:T(8,128)(2,1)S(1)}, bf16[48,8,128]{2,0,1:T(8,128)(2,1)S(1)}, u32[]{:S(2)}, u32[]{:S(2)}) collective-permute-start(bf16[48,8,128]{2,0,1:T(8,128)(2,1)S(1)} %get-tuple-element.27), channel_id=1, source_target_pairs={{8,0},{16,8},{24,16},{32,24},{40,32},{48,40},{56,48},{64,56},{72,6... | collective-permute-start | bytes 294920 | tf_op jit(solution)/shard_map/ppermute | solution.py:17
  11.6 2.0 %collective-permute-done.1 = bf16[48,8,128]{2,0,1:T(8,128)(2,1)S(1)} collective-permute-done((bf16[48,8,128]{2,0,1:T(8,128)(2,1)S(1)}, bf16[48,8,128]{2,0,1:T(8,128)(2,1)S(1)}, u32[]{:S(2)}, u32[]{:S(2)}) %collective-permute-start.1) | collective-permute-done | bytes 98336 | tf_op jit(solution)/shard_map/ppermute | solution.py:17
  13.9 0.5 copy.54
  14.4 4.0 %collective-permute-start.2 = (bf16[48,48,8]{1,2,0:T(8,128)(2,1)S(1)}, bf16[48,48,8]{1,2,0:T(8,128)(2,1)S(1)}, u32[]{:S(2)}, u32[]{:S(2)}) collective-permute-start(bf16[48,48,8]{1,2,0:T(8,128)(2,1)S(1)} %copy.54), channel_id=1, source_target_pairs={{0,1},{1,2},{2,3},{3,4},{4,5},{5,6},{6,7},{8,9},{9,10},{10,11},{11... | collective-permute-start | bytes 110600 | tf_op jit(solution)/shard_map/ppermute | solution.py:16
  18.4 0.5 copy.56
  19.0 3.3 %collective-permute-start.3 = (bf16[48,48,8]{1,2,0:T(8,128)(2,1)S(1)}, bf16[48,48,8]{1,2,0:T(8,128)(2,1)S(1)}, u32[]{:S(2)}, u32[]{:S(2)}) collective-permute-start(bf16[48,48,8]{1,2,0:T(8,128)(2,1)S(1)} %copy.56), channel_id=1, source_target_pairs={{1,0},{2,1},{3,2},{4,3},{5,4},{6,5},{7,6},{9,8},{10,9},{11,10},{12... | collective-permute-start | bytes 110600 | tf_op jit(solution)/shard_map/ppermute | solution.py:17
  22.3 0.9 copy.74
  23.2 7.4 %all-to-all-start.3 = ((bf16[48,32,128]{2,0,1:T(8,128)(2,1)}), bf16[48,32,128]{2,0,1:T(8,128)(2,1)S(1)}, u32[]{:S(2)}, u32[]{:S(2)}) async-start(bf16[48,32,128]{2,0,1:T(8,128)(2,1)} %copy.74), calls=%async_computation.3 | async-start | bytes 786432 | tf_op jit(solution)/shard_map/all_to_all | solution.py:68
  31.1 0.5 copy.57
  31.6 0.8 pad_maximum_fusion
  32.9 0.5 copy-done.3
  34.3 1.7 copy-done.5
  36.0 0.8 fusion.8
  36.8 1.1 fusion.7
  37.9 7.2 %all-to-all-start = ((bf16[48,32,128]{2,0,1:T(8,128)(2,1)}), bf16[48,32,128]{2,0,1:T(8,128)(2,1)S(1)}, u32[]{:S(2)}, u32[]{:S(2)}) async-start(bf16[48,32,128]{2,0,1:T(8,128)(2,1)} %fusion.7), calls=%async_computation | async-start | bytes 786432 | tf_op jit(solution)/shard_map/all_to_all | solution.py:68
  45.1 0.7 copy.77
  45.7 2.5 %reshape.68 = bf16[32,2,3072]{2,1,0:T(2,128)(2,1)} reshape(bf16[1024,4,48]{2,1,0:T(4,128)(2,1)S(1)} %bitcast.198) | data formatting | bytes 786432
  48.2 3.7 %all-to-all-done = bf16[48,32,128]{2,0,1:T(8,128)(2,1)S(1)} async-done(((bf16[48,32,128]{2,0,1:T(8,128)(2,1)}), bf16[48,32,128]{2,0,1:T(8,128)(2,1)S(1)}, u32[]{:S(2)}, u32[]{:S(2)}) %all-to-all-start) | async-done | bytes 393248 | tf_op jit(solution)/shard_map/all_to_all | solution.py:68
  51.9 7.5 %all-to-all-start.4 = ((bf16[32,2,3072]{2,1,0:T(2,128)(2,1)}), bf16[32,2,3072]{2,1,0:T(2,128)(2,1)S(1)}, u32[]{:S(2)}, u32[]{:S(2)}) async-start(bf16[32,2,3072]{2,1,0:T(2,128)(2,1)} %reshape.68), calls=%async_computation.4 | async-start | bytes 786432 | tf_op jit(solution)/shard_map/all_to_all | solution.py:69
  59.4 0.7 copy.95
  60.1 2.5 %reshape.64 = bf16[32,2,3072]{2,1,0:T(2,128)(2,1)} reshape(bf16[1024,4,48]{2,1,0:T(4,128)(2,1)S(1)} %bitcast.199) | data formatting | bytes 786432
  62.5 11.4 %all-to-all-done.4 = bf16[32,2,3072]{2,1,0:T(2,128)(2,1)S(1)} async-done(((bf16[32,2,3072]{2,1,0:T(2,128)(2,1)}), bf16[32,2,3072]{2,1,0:T(2,128)(2,1)S(1)}, u32[]{:S(2)}, u32[]{:S(2)}) %all-to-all-start.4) | async-done | bytes 393248 | tf_op jit(solution)/shard_map/all_to_all | solution.py:69
  73.9 5.2 %all-to-all-start.1 = ((bf16[32,2,3072]{2,1,0:T(2,128)(2,1)}), bf16[32,2,3072]{2,1,0:T(2,128)(2,1)S(1)}, u32[]{:S(2)}, u32[]{:S(2)}) async-start(bf16[32,2,3072]{2,1,0:T(2,128)(2,1)} %reshape.64), calls=%async_computation.1 | async-start | bytes 786432 | tf_op jit(solution)/shard_map/all_to_all | solution.py:69
  79.1 1.1 reshape.69
  80.4 2.3 %reshape.70 = bf16[8,2,12288]{2,1,0:T(2,128)(2,1)} reshape(bf16[32,4,32,48]{3,2,1,0:T(8,128)(2,1)S(1)} %bitcast.201) | data formatting | bytes 786432
  82.7 10.8 %all-to-all-done.1 = bf16[32,2,3072]{2,1,0:T(2,128)(2,1)S(1)} async-done(((bf16[32,2,3072]{2,1,0:T(2,128)(2,1)}), bf16[32,2,3072]{2,1,0:T(2,128)(2,1)S(1)}, u32[]{:S(2)}, u32[]{:S(2)}) %all-to-all-start.1) | async-done | bytes 393248 | tf_op jit(solution)/shard_map/all_to_all | solution.py:69
  93.5 6.0 %all-to-all-start.5 = ((bf16[8,2,12288]{2,1,0:T(2,128)(2,1)}), bf16[8,2,12288]{2,1,0:T(2,128)(2,1)S(1)}, u32[]{:S(2)}, u32[]{:S(2)}) async-start(bf16[8,2,12288]{2,1,0:T(2,128)(2,1)} %reshape.70), calls=%async_computation.5 | async-start | bytes 786432 | tf_op jit(solution)/shard_map/all_to_all | solution.py:71
  99.5 1.1 reshape.65
  100.8 2.3 %reshape.66 = bf16[8,2,12288]{2,1,0:T(2,128)(2,1)} reshape(bf16[32,4,32,48]{3,2,1,0:T(8,128)(2,1)S(1)} %bitcast.203) | data formatting | bytes 786432
  103.1 3.3 %all-to-all-done.5 = bf16[8,2,12288]{2,1,0:T(2,128)(2,1)S(1)} async-done(((bf16[8,2,12288]{2,1,0:T(2,128)(2,1)}), bf16[8,2,12288]{2,1,0:T(2,128)(2,1)S(1)}, u32[]{:S(2)}, u32[]{:S(2)}) %all-to-all-start.5) | async-done | bytes 393248 | tf_op jit(solution)/shard_map/all_to_all | solution.py:71
  106.4 6.7 %all-to-all-start.2 = ((bf16[8,2,12288]{2,1,0:T(2,128)(2,1)}), bf16[8,2,12288]{2,1,0:T(2,128)(2,1)}, u32[]{:S(2)}, u32[]{:S(2)}) async-start(bf16[8,2,12288]{2,1,0:T(2,128)(2,1)} %reshape.66), calls=%async_computation.2 | async-start | bytes 786432 | tf_op jit(solution)/shard_map/all_to_all | solution.py:71
  113.0 1.1 reshape.71
  114.6 1.3 copy.81
  115.9 1.5 fusion.6
  117.4 1.4 convolution_bitcast_fusion.4
  118.8 1.0 convolution_bitcast_fusion.3
  120.1 1.9 %collective-permute-start.4 = (bf16[48,8,128]{2,0,1:T(8,128)(2,1)S(1)}, bf16[48,8,128]{2,0,1:T(8,128)(2,1)S(1)}, u32[]{:S(2)}, u32[]{:S(2)}) collective-permute-start(bf16[48,8,128]{2,0,1:T(8,128)(2,1)S(1)} %get-tuple-element.24), channel_id=1, source_target_pairs={{0,8},{8,16},{16,24},{24,32},{32,40},{40,48},{48,56},{56,64},{64,7... | collective-permute-start | bytes 294920 | tf_op jit(solution)/shard_map/ppermute | solution.py:16
  122.0 5.8 %collective-permute-start.5 = (bf16[48,8,128]{2,0,1:T(8,128)(2,1)S(1)}, bf16[48,8,128]{2,0,1:T(8,128)(2,1)S(1)}, u32[]{:S(2)}, u32[]{:S(2)}) collective-permute-start(bf16[48,8,128]{2,0,1:T(8,128)(2,1)S(1)} %get-tuple-element.25), channel_id=1, source_target_pairs={{8,0},{16,8},{24,16},{32,24},{40,32},{48,40},{56,48},{64,56},{72,6... | collective-permute-start | bytes 294920 | tf_op jit(solution)/shard_map/ppermute | solution.py:17
  128.2 1.8 %collective-permute-done.5 = bf16[48,8,128]{2,0,1:T(8,128)(2,1)S(1)} collective-permute-done((bf16[48,8,128]{2,0,1:T(8,128)(2,1)S(1)}, bf16[48,8,128]{2,0,1:T(8,128)(2,1)S(1)}, u32[]{:S(2)}, u32[]{:S(2)}) %collective-permute-start.5) | collective-permute-done | bytes 98336 | tf_op jit(solution)/shard_map/ppermute | solution.py:17
  130.3 0.5 copy.82
  130.8 2.0 %collective-permute-start.6 = (bf16[48,48,8]{1,2,0:T(8,128)(2,1)S(1)}, bf16[48,48,8]{1,2,0:T(8,128)(2,1)S(1)}, u32[]{:S(2)}, u32[]{:S(2)}) collective-permute-start(bf16[48,48,8]{1,2,0:T(8,128)(2,1)S(1)} %copy.82), channel_id=1, source_target_pairs={{1,0},{2,1},{3,2},{4,3},{5,4},{6,5},{7,6},{9,8},{10,9},{11,10},{12... | collective-permute-start | bytes 110600 | tf_op jit(solution)/shard_map/ppermute | solution.py:17
  132.9 0.5 copy.84
  133.4 6.2 %collective-permute-start.7 = (bf16[48,48,8]{1,2,0:T(8,128)(2,1)S(1)}, bf16[48,48,8]{1,2,0:T(8,128)(2,1)S(1)}, u32[]{:S(2)}, u32[]{:S(2)}) collective-permute-start(bf16[48,48,8]{1,2,0:T(8,128)(2,1)S(1)} %copy.84), channel_id=1, source_target_pairs={{0,1},{1,2},{2,3},{3,4},{4,5},{5,6},{6,7},{8,9},{9,10},{10,11},{11... | collective-permute-start | bytes 110600 | tf_op jit(solution)/shard_map/ppermute | solution.py:16
  140.5 1.3 collective-permute-done.7
  142.3 0.8 maximum_maximum_fusion.1
  143.9 0.6 collective-permute-done.9
  144.9 6.2 %collective-permute-done.10 = f32[180,128]{1,0:T(8,128)S(1)} collective-permute-done((f32[180,128]{1,0:T(8,128)S(1)}, f32[180,128]{1,0:T(8,128)S(1)}, u32[]{:S(2)}, u32[]{:S(2)}) %collective-permute-start.10) | collective-permute-done | bytes 92192 | tf_op jit(solution)/shard_map/ppermute | solution.py:59
  151.3 6.6 %collective-permute-done.11 = f32[180,128]{1,0:T(8,128)S(1)} collective-permute-done((f32[180,128]{1,0:T(8,128)S(1)}, f32[180,128]{1,0:T(8,128)S(1)}, u32[]{:S(2)}, u32[]{:S(2)}) %collective-permute-start.11) | collective-permute-done | bytes 92192 | tf_op jit(solution)/shard_map/ppermute | solution.py:59
  158.1 4.5 %collective-permute-done.12 = f32[180,128]{1,0:T(8,128)S(1)} collective-permute-done((f32[180,128]{1,0:T(8,128)S(1)}, f32[180,128]{1,0:T(8,128)S(1)}, u32[]{:S(2)}, u32[]{:S(2)}) %collective-permute-start.12) | collective-permute-done | bytes 92192 | tf_op jit(solution)/shard_map/ppermute | solution.py:59
  162.7 1.7 fusion.4
  164.4 2.3 %reshape.67 = bf16[32,4,32,48]{3,2,1,0:T(8,128)(2,1)S(1)} reshape(bf16[8,2,12288]{2,1,0:T(2,128)(2,1)} %all-to-all-done.2) | data formatting | bytes 786432
  166.6 2.1 %collective-permute-done.13 = f32[180,128]{1,0:T(8,128)S(1)} collective-permute-done((f32[180,128]{1,0:T(8,128)S(1)}, f32[180,128]{1,0:T(8,128)S(1)}, u32[]{:S(2)}, u32[]{:S(2)}) %collective-permute-start.13) | collective-permute-done | bytes 92192 | tf_op jit(solution)/shard_map/ppermute | solution.py:59
  168.7 3.0 %collective-permute-start.14 = (f32[180,128]{1,0:T(8,128)S(1)}, f32[180,128]{1,0:T(8,128)}, u32[]{:S(2)}, u32[]{:S(2)}) collective-permute-start(f32[180,128]{1,0:T(8,128)S(1)} %add.45), channel_id=1, source_target_pairs={{0,2},{1,3},{2,0},{3,1},{4,6},{5,7},{6,4},{7,5},{8,10},{9,11},{10,... | collective-permute-start | bytes 276488 | tf_op jit(solution)/shard_map/ppermute | solution.py:59
  172.3 1.3 copy.73
  173.6 0.8 collective-permute-done.14
  174.4 0.9 add.46
  175.3 3.3 %collective-permute-start.15 = (f32[180,128]{1,0:T(8,128)S(1)}, f32[180,128]{1,0:T(8,128)S(1)}, u32[]{:S(2)}, u32[]{:S(2)}) collective-permute-start(f32[180,128]{1,0:T(8,128)S(1)} %add.46), channel_id=1, source_target_pairs={{0,6},{1,7},{2,4},{3,5},{4,2},{5,3},{6,0},{7,1},{8,14},{9,15},{10,... | collective-permute-start | bytes 276488 | tf_op jit(solution)/shard_map/ppermute | solution.py:59
  178.6 1.2 add_convert_fusion
  179.8 0.8 copy.87
  180.7 0.8 copy.86
  181.6 0.8 div.18
  182.4 0.7 div.21
  (76 shorter events, 7.6 us)
Async XLA Ops:
  0.6 33.6 %copy-start = (bf16[3,3,48,48]{3,2,1,0:T(8,128)(2,1)S(1)}, bf16[3,3,48,48]{3,2,1,0:T(8,128)(2,1)}, u32[]{:S(2)}) copy-start(bf16[3,3,48,48]{3,2,1,0:T(8,128)(2,1)} %param.5) | copy-start | bytes 124420
  1.8 9.8 %collective-permute-start = (bf16[48,8,128]{2,0,1:T(8,128)(2,1)S(1)}, bf16[48,8,128]{2,0,1:T(8,128)(2,1)S(1)}, u32[]{:S(2)}, u32[]{:S(2)}) collective-permute-start(bf16[48,8,128]{2,0,1:T(8,128)(2,1)S(1)} %get-tuple-element.26), channel_id=1, source_target_pairs={{0,8},{8,16},{16,24},{24,32},{32,40},{40,48},{48,56},{56,64},{64,7... | collective-permute-start | bytes 294920 | tf_op jit(solution)/shard_map/ppermute | solution.py:16
  3.8 18.5 %copy-start.1 = (bf16[48,32,128]{2,1,0:T(8,128)(2,1)S(1)}, bf16[48,32,128]{2,1,0:T(8,128)(2,1)}, u32[]{:S(2)}) copy-start(bf16[48,32,128]{2,1,0:T(8,128)(2,1)} %param.7) | copy-start | bytes 1179652
  3.8 9.8 %collective-permute-start.1 = (bf16[48,8,128]{2,0,1:T(8,128)(2,1)S(1)}, bf16[48,8,128]{2,0,1:T(8,128)(2,1)S(1)}, u32[]{:S(2)}, u32[]{:S(2)}) collective-permute-start(bf16[48,8,128]{2,0,1:T(8,128)(2,1)S(1)} %get-tuple-element.27), channel_id=1, source_target_pairs={{8,0},{16,8},{24,16},{32,24},{40,32},{48,40},{56,48},{64,56},{72,6... | collective-permute-start | bytes 294920 | tf_op jit(solution)/shard_map/ppermute | solution.py:17
  14.4 16.2 %collective-permute-start.2 = (bf16[48,48,8]{1,2,0:T(8,128)(2,1)S(1)}, bf16[48,48,8]{1,2,0:T(8,128)(2,1)S(1)}, u32[]{:S(2)}, u32[]{:S(2)}) collective-permute-start(bf16[48,48,8]{1,2,0:T(8,128)(2,1)S(1)} %copy.54), channel_id=1, source_target_pairs={{0,1},{1,2},{2,3},{3,4},{4,5},{5,6},{6,7},{8,9},{9,10},{10,11},{11... | collective-permute-start | bytes 110600 | tf_op jit(solution)/shard_map/ppermute | solution.py:16
  19.0 12.1 %collective-permute-start.3 = (bf16[48,48,8]{1,2,0:T(8,128)(2,1)S(1)}, bf16[48,48,8]{1,2,0:T(8,128)(2,1)S(1)}, u32[]{:S(2)}, u32[]{:S(2)}) collective-permute-start(bf16[48,48,8]{1,2,0:T(8,128)(2,1)S(1)} %copy.56), channel_id=1, source_target_pairs={{1,0},{2,1},{3,2},{4,3},{5,4},{6,5},{7,6},{9,8},{10,9},{11,10},{12... | collective-permute-start | bytes 110600 | tf_op jit(solution)/shard_map/ppermute | solution.py:17
  23.2 14.7 %all-to-all-start.3 = ((bf16[48,32,128]{2,0,1:T(8,128)(2,1)}), bf16[48,32,128]{2,0,1:T(8,128)(2,1)S(1)}, u32[]{:S(2)}, u32[]{:S(2)}) async-start(bf16[48,32,128]{2,0,1:T(8,128)(2,1)} %copy.74), calls=%async_computation.3 | async-start | bytes 786432 | tf_op jit(solution)/shard_map/all_to_all | solution.py:68
  32.4 1.0 copy-start.3
  34.0 2.8 %copy-start.8 = (bf16[48,48]{1,0:T(8,128)(2,1)S(1)}, bf16[48,48]{1,0:T(8,128)(2,1)}, u32[]{:S(2)}) copy-start(bf16[48,48]{1,0:T(8,128)(2,1)} %param.6) | copy-start | bytes 13828
  34.3 1.7 copy-start.5
  37.9 14.0 %all-to-all-start = ((bf16[48,32,128]{2,0,1:T(8,128)(2,1)}), bf16[48,32,128]{2,0,1:T(8,128)(2,1)S(1)}, u32[]{:S(2)}, u32[]{:S(2)}) async-start(bf16[48,32,128]{2,0,1:T(8,128)(2,1)} %fusion.7), calls=%async_computation | async-start | bytes 786432 | tf_op jit(solution)/shard_map/all_to_all | solution.py:68
  51.9 22.0 %all-to-all-start.4 = ((bf16[32,2,3072]{2,1,0:T(2,128)(2,1)}), bf16[32,2,3072]{2,1,0:T(2,128)(2,1)S(1)}, u32[]{:S(2)}, u32[]{:S(2)}) async-start(bf16[32,2,3072]{2,1,0:T(2,128)(2,1)} %reshape.68), calls=%async_computation.4 | async-start | bytes 786432 | tf_op jit(solution)/shard_map/all_to_all | solution.py:69
  73.9 19.6 %all-to-all-start.1 = ((bf16[32,2,3072]{2,1,0:T(2,128)(2,1)}), bf16[32,2,3072]{2,1,0:T(2,128)(2,1)S(1)}, u32[]{:S(2)}, u32[]{:S(2)}) async-start(bf16[32,2,3072]{2,1,0:T(2,128)(2,1)} %reshape.64), calls=%async_computation.1 | async-start | bytes 786432 | tf_op jit(solution)/shard_map/all_to_all | solution.py:69
  93.5 12.9 %all-to-all-start.5 = ((bf16[8,2,12288]{2,1,0:T(2,128)(2,1)}), bf16[8,2,12288]{2,1,0:T(2,128)(2,1)S(1)}, u32[]{:S(2)}, u32[]{:S(2)}) async-start(bf16[8,2,12288]{2,1,0:T(2,128)(2,1)} %reshape.70), calls=%async_computation.5 | async-start | bytes 786432 | tf_op jit(solution)/shard_map/all_to_all | solution.py:71
  106.4 58.0 %all-to-all-start.2 = ((bf16[8,2,12288]{2,1,0:T(2,128)(2,1)}), bf16[8,2,12288]{2,1,0:T(2,128)(2,1)}, u32[]{:S(2)}, u32[]{:S(2)}) async-start(bf16[8,2,12288]{2,1,0:T(2,128)(2,1)} %reshape.66), calls=%async_computation.2 | async-start | bytes 786432 | tf_op jit(solution)/shard_map/all_to_all | solution.py:71
  115.9 2.9 %copy-start.6 = (bf16[9,48,32,128]{3,1,0,2:T(8,128)(2,1)S(1)}, bf16[9,48,32,128]{3,1,0,2:T(8,128)(2,1)}, u32[]{:S(2)}) copy-start(bf16[9,48,32,128]{3,1,0,2:T(8,128)(2,1)} %copy-done.5) | copy-start | bytes 10616836
  120.1 8.0 %collective-permute-start.4 = (bf16[48,8,128]{2,0,1:T(8,128)(2,1)S(1)}, bf16[48,8,128]{2,0,1:T(8,128)(2,1)S(1)}, u32[]{:S(2)}, u32[]{:S(2)}) collective-permute-start(bf16[48,8,128]{2,0,1:T(8,128)(2,1)S(1)} %get-tuple-element.24), channel_id=1, source_target_pairs={{0,8},{8,16},{16,24},{24,32},{32,40},{40,48},{48,56},{56,64},{64,7... | collective-permute-start | bytes 294920 | tf_op jit(solution)/shard_map/ppermute | solution.py:16
  122.0 8.0 %collective-permute-start.5 = (bf16[48,8,128]{2,0,1:T(8,128)(2,1)S(1)}, bf16[48,8,128]{2,0,1:T(8,128)(2,1)S(1)}, u32[]{:S(2)}, u32[]{:S(2)}) collective-permute-start(bf16[48,8,128]{2,0,1:T(8,128)(2,1)S(1)} %get-tuple-element.25), channel_id=1, source_target_pairs={{8,0},{16,8},{24,16},{32,24},{40,32},{48,40},{56,48},{64,56},{72,6... | collective-permute-start | bytes 294920 | tf_op jit(solution)/shard_map/ppermute | solution.py:17
  127.8 11.8 %collective-permute-start.8 = (f32[180,128]{1,0:T(8,128)S(1)}, f32[180,128]{1,0:T(8,128)S(1)}, u32[]{:S(2)}, u32[]{:S(2)}) collective-permute-start(f32[180,128]{1,0:T(8,128)S(1)} %maximum_bitcast_fusion), channel_id=1, source_target_pairs={{0,8},{8,0},{16,24},{24,16},{32,40},{40,32},{48,56},{56,48},{64,72... | collective-permute-start | bytes 276488 | tf_op jit(solution)/shard_map/ppermute | solution.py:59
  130.8 9.2 %collective-permute-start.6 = (bf16[48,48,8]{1,2,0:T(8,128)(2,1)S(1)}, bf16[48,48,8]{1,2,0:T(8,128)(2,1)S(1)}, u32[]{:S(2)}, u32[]{:S(2)}) collective-permute-start(bf16[48,48,8]{1,2,0:T(8,128)(2,1)S(1)} %copy.82), channel_id=1, source_target_pairs={{1,0},{2,1},{3,2},{4,3},{5,4},{6,5},{7,6},{9,8},{10,9},{11,10},{12... | collective-permute-start | bytes 110600 | tf_op jit(solution)/shard_map/ppermute | solution.py:17
  133.4 8.4 %collective-permute-start.7 = (bf16[48,48,8]{1,2,0:T(8,128)(2,1)S(1)}, bf16[48,48,8]{1,2,0:T(8,128)(2,1)S(1)}, u32[]{:S(2)}, u32[]{:S(2)}) collective-permute-start(bf16[48,48,8]{1,2,0:T(8,128)(2,1)S(1)} %copy.84), channel_id=1, source_target_pairs={{0,1},{1,2},{2,3},{3,4},{4,5},{5,6},{6,7},{8,9},{9,10},{10,11},{11... | collective-permute-start | bytes 110600 | tf_op jit(solution)/shard_map/ppermute | solution.py:16
  139.6 4.9 %collective-permute-start.9 = (f32[180,128]{1,0:T(8,128)S(1)}, f32[180,128]{1,0:T(8,128)S(1)}, u32[]{:S(2)}, u32[]{:S(2)}) collective-permute-start(f32[180,128]{1,0:T(8,128)S(1)} %fusion.51), channel_id=1, source_target_pairs={{0,16},{8,24},{16,0},{24,8},{32,48},{40,56},{48,32},{56,40},{64,80... | collective-permute-start | bytes 276488 | tf_op jit(solution)/shard_map/ppermute | solution.py:59
  143.7 18.9 %copy-start.2 = (bf16[48,32,128]{2,1,0:T(8,128)(2,1)S(1)}, bf16[48,32,128]{2,1,0:T(8,128)(2,1)}, u32[]{:S(2)}) copy-start(bf16[48,32,128]{2,1,0:T(8,128)(2,1)} %param.7) | copy-start | bytes 1179652
  143.8 18.9 %copy-start.4 = (bf16[48,32,128]{2,1,0:T(8,128)(2,1)S(1)}, bf16[48,32,128]{2,1,0:T(8,128)(2,1)}, u32[]{:S(2)}) copy-start(bf16[48,32,128]{2,1,0:T(8,128)(2,1)} %param.4) | copy-start | bytes 1179652
  144.5 6.6 %collective-permute-start.10 = (f32[180,128]{1,0:T(8,128)S(1)}, f32[180,128]{1,0:T(8,128)S(1)}, u32[]{:S(2)}, u32[]{:S(2)}) collective-permute-start(f32[180,128]{1,0:T(8,128)S(1)} %fusion.52), channel_id=1, source_target_pairs={{0,48},{8,56},{16,32},{24,40},{32,16},{40,24},{48,0},{56,8},{64,11... | collective-permute-start | bytes 276488 | tf_op jit(solution)/shard_map/ppermute | solution.py:59
  151.1 6.8 %collective-permute-start.11 = (f32[180,128]{1,0:T(8,128)S(1)}, f32[180,128]{1,0:T(8,128)S(1)}, u32[]{:S(2)}, u32[]{:S(2)}) collective-permute-start(f32[180,128]{1,0:T(8,128)S(1)} %add.42), channel_id=1, source_target_pairs={{0,96},{8,104},{16,112},{24,120},{32,64},{40,72},{48,80},{56,88},{... | collective-permute-start | bytes 276488 | tf_op jit(solution)/shard_map/ppermute | solution.py:59
  157.9 4.7 %collective-permute-start.12 = (f32[180,128]{1,0:T(8,128)S(1)}, f32[180,128]{1,0:T(8,128)S(1)}, u32[]{:S(2)}, u32[]{:S(2)}) collective-permute-start(f32[180,128]{1,0:T(8,128)S(1)} %add.43), channel_id=1, source_target_pairs={{0,128},{8,136},{16,144},{24,152},{32,160},{40,168},{48,176},{56,1... | collective-permute-start | bytes 276488 | tf_op jit(solution)/shard_map/ppermute | solution.py:59
  162.6 6.2 %collective-permute-start.13 = (f32[180,128]{1,0:T(8,128)S(1)}, f32[180,128]{1,0:T(8,128)S(1)}, u32[]{:S(2)}, u32[]{:S(2)}) collective-permute-start(f32[180,128]{1,0:T(8,128)S(1)} %add.44), channel_id=1, source_target_pairs={{0,1},{1,0},{2,3},{3,2},{4,5},{5,4},{6,7},{7,6},{8,9},{9,8},{10,11... | collective-permute-start | bytes 276488 | tf_op jit(solution)/shard_map/ppermute | solution.py:59
  168.7 5.7 %collective-permute-start.14 = (f32[180,128]{1,0:T(8,128)S(1)}, f32[180,128]{1,0:T(8,128)}, u32[]{:S(2)}, u32[]{:S(2)}) collective-permute-start(f32[180,128]{1,0:T(8,128)S(1)} %add.45), channel_id=1, source_target_pairs={{0,2},{1,3},{2,0},{3,1},{4,6},{5,7},{6,4},{7,5},{8,10},{9,11},{10,... | collective-permute-start | bytes 276488 | tf_op jit(solution)/shard_map/ppermute | solution.py:59
  173.6 6.3 %copy-start.7 = (bf16[48,32,128]{2,0,1:T(8,128)(2,1)S(1)}, bf16[48,32,128]{2,0,1:T(8,128)(2,1)}, u32[]{:S(2)}) copy-start(bf16[48,32,128]{2,0,1:T(8,128)(2,1)} %fusion.4) | copy-start | bytes 1179652
  175.3 6.2 %collective-permute-start.15 = (f32[180,128]{1,0:T(8,128)S(1)}, f32[180,128]{1,0:T(8,128)S(1)}, u32[]{:S(2)}, u32[]{:S(2)}) collective-permute-start(f32[180,128]{1,0:T(8,128)S(1)} %add.46), channel_id=1, source_target_pairs={{0,6},{1,7},{2,4},{3,5},{4,2},{5,3},{6,0},{7,1},{8,14},{9,15},{10,... | collective-permute-start | bytes 276488 | tf_op jit(solution)/shard_map/ppermute | solution.py:59
